TPU v7x, 256 devices: a whole 4x4x8 slice. The times are simulated.
256 devices in a mesh: dp: 8 (over x, core), seq: 32 (over y, z).
Axes of the slice: x: 4, y: 4, z: 8, core: 2. Of those that a mesh axis runs over, the one named last changes fastest.
Arguments:
- queries: bfloat16 [8, 8192, 4096], P('dp', 'seq'), may hold values from -51 to 51
- keys: bfloat16 [8, 8192, 512], P('dp', 'seq'), may hold values from -6 to 6
- values: bfloat16 [8, 8192, 512], P('dp', 'seq'), may hold values from -6 to 6
- targets: bfloat16 [8, 8192, 4096], P('dp', 'seq'), may hold values from -6 to 6
- q_map: bfloat16 [32, 128, 128], replicated, may hold values from -1.5 to 1.5
- k_map: bfloat16 [4, 128, 128], replicated, may hold values from -1.5 to 1.5
- doc_spans: int32 [8, 8], P('dp'), may hold values from 1 to 24, 64 in all within a row
Outputs:
- grad_q_map: float32 [32, 128, 128], replicated
- grad_k_map: float32 [4, 128, 128], replicated
Inputs may be any that keep to these rules, and one draw needn't show every extreme that they name: `doc_spans`: each row sums to 64, and the longest document has exactly 24 blocks.
All inputs are finite; a program needn't handle non-finite values.
Results may differ from a plain program's by a relative error of at most 0.006.
The roundings to bfloat16 on the way count: a program that leaves them out, or rounds other values in their place, can miss the bound.
Values sent between devices are 32-bit elements; how exact they have to be, the bound alone decides.
A program may use at most 128 MiB of HBM per device.

v0:
```python
import math

import jax
import jax.numpy as jnp
from jax import lax
from jax.sharding import Mesh
from jax.sharding import PartitionSpec as P

SPAN = 128
SEQ = ("seq_0", "seq_1")


def filled_with(shard, identity):
    return jax.tree.map(
        lambda part, zero: jnp.zeros_like(part) + jnp.asarray(zero, part.dtype), shard, identity
    )


def carried_in_2(shard, axes, combine, identity, reverse):
    before = start = filled_with(shard, identity)
    total = shard
    for axis in reversed(axes):
        count, index = (lax.axis_size(axis), lax.axis_index(axis))
        pieces = jax.tree.map(lambda part: lax.all_gather(part, axis), total)
        inside, total = (start, start)
        for k in reversed(range(count)) if reverse else range(count):
            passed = k > index if reverse else k < index
            total = combine(total, jax.tree.map(lambda part: part[k], pieces))
            inside = jax.tree.map(lambda new, old: jnp.where(passed, new, old), total, inside)
        before = combine(inside, before)
    return before


def in_blocks(shard, dim, count):
    before, after = (shard.shape[:dim], shard.shape[dim + 1 :])
    return jnp.moveaxis(shard.reshape(*before, count, -1, *after), dim, 0)


def sum_at_owner(shard, axis, dim):
    blocks = in_blocks(shard, dim, lax.axis_size(axis))
    arrived = lax.all_to_all(blocks, axis, split_axis=0, concat_axis=0, tiled=True)
    return arrived.sum(axis=0)


def gathered_total(shard, axis):
    blocks = lax.all_gather(shard, axis)
    return blocks.sum(axis=0)


def sent_to_all(shard, axis):
    copies = jnp.broadcast_to(shard, (lax.axis_size(axis), *shard.shape))
    return lax.all_to_all(copies, axis, split_axis=0, concat_axis=0, tiled=True)


def laid_out(blocks, dim):
    blocks = jnp.moveaxis(blocks, 0, dim)
    lengths = blocks.shape
    return blocks.reshape(*lengths[:dim], lengths[dim] * lengths[dim + 1], *lengths[dim + 2 :])


def gather_directly(shard, axis, dim):
    blocks = sent_to_all(shard, axis)
    return laid_out(blocks, dim)


def hedgehog(inputs, weight, form):
    mapped = jnp.einsum(form, inputs, weight, preferred_element_type=jnp.float32)
    upper = jax.nn.softmax(mapped, axis=-1)
    lower = jax.nn.softmax(-mapped, axis=-1)
    return (upper, lower, jnp.concatenate([upper, lower], axis=-1).astype(jnp.bfloat16))


def map_grad(upper, lower, grad, width):
    grad_up = grad[..., :width]
    grad_low = grad[..., width:]
    first = upper * (grad_up - jnp.sum(upper * grad_up, -1, keepdims=True))
    second = lower * (grad_low - jnp.sum(lower * grad_low, -1, keepdims=True))
    return (first - second).astype(jnp.bfloat16)


def span_middle(feat_q, feat_k, vals, tgt, state_b, norm_b, coef):
    size = feat_q.shape[1]
    causal = jnp.tril(jnp.ones((size, size), jnp.bool_))
    scores = jnp.einsum("ncxgf,nsxf->nxgcs", feat_q, feat_k, preferred_element_type=jnp.float32)
    scores = jnp.where(causal, scores, 0.0)
    local_den = jnp.transpose(jnp.sum(scores, -1), (0, 3, 1, 2))
    numer = jnp.einsum(
        "nxgcs,nsxd->ncxgd", scores.astype(jnp.bfloat16), vals, preferred_element_type=jnp.float32
    )
    numer = numer + jnp.einsum(
        "ncxgf,nxfd->ncxgd", feat_q, state_b, preferred_element_type=jnp.float32
    )
    denom = local_den + jnp.einsum(
        "ncxgf,nxf->ncxg", feat_q, norm_b, preferred_element_type=jnp.float32
    )
    output = numer / denom[..., None]
    d_out = coef * (output - tgt.astype(jnp.float32))
    d_numer = (d_out / denom[..., None]).astype(jnp.bfloat16)
    d_denom = -jnp.sum(d_out * output, -1) / denom
    pairs = jnp.einsum("ncxgd,nsxd->nxgcs", d_numer, vals, preferred_element_type=jnp.float32)
    pairs = pairs + jnp.transpose(d_denom, (0, 2, 3, 1))[..., None]
    pairs = jnp.where(causal, pairs, 0.0).astype(jnp.bfloat16)
    d_feat_q = jnp.einsum("nxgcs,nsxf->ncxgf", pairs, feat_k, preferred_element_type=jnp.float32)
    d_feat_q = d_feat_q + jnp.einsum(
        "ncxgd,nxfd->ncxgf", d_numer, state_b, preferred_element_type=jnp.float32
    )
    d_feat_q = d_feat_q + d_denom[..., None] * norm_b.astype(jnp.float32)[:, None, :, None, :]
    back_state = jnp.einsum(
        "ncxgf,ncxgd->nxfd", feat_q, d_numer, preferred_element_type=jnp.float32
    )
    back_norm = jnp.sum(feat_q.astype(jnp.float32) * d_denom[..., None], axis=(1, 3))
    return (pairs, d_feat_q, back_state, back_norm)


def span_last(pairs, feat_q, vals, rstate_b, rnorm_b):
    d_feat_k = jnp.einsum("nxgcs,ncxgf->nsxf", pairs, feat_q, preferred_element_type=jnp.float32)
    d_feat_k = d_feat_k + jnp.einsum(
        "nsxd,nxfd->nsxf", vals, rstate_b, preferred_element_type=jnp.float32
    )
    return d_feat_k + rnorm_b.astype(jnp.float32)[:, None, :, :]


def reset_join(earlier, later):
    keep = 1.0 - later[2]
    return (
        later[0] + keep * earlier[0],
        later[1] + keep * earlier[1],
        jnp.maximum(earlier[2], later[2]),
    )


def spread_blocks(weights, blocks):
    return jnp.einsum("cy,y...->c...", weights, blocks, precision=lax.Precision.HIGHEST)


def shards(queries, keys, values, targets, q_map, k_map, doc_spans):
    hq = q_map.shape[0]
    hd = q_map.shape[1]
    hk = k_map.shape[0]
    group = hq // hk
    tok_rows = queries.shape[1]
    count = tok_rows // SPAN
    coef = 2.0 / math.sqrt(lax.axis_size("dp") * lax.axis_size(SEQ) * tok_rows * hd)
    q_heads = queries.reshape(count, SPAN, hq, hd)
    k_heads = keys.reshape(count, SPAN, hk, hd)
    vals = values.reshape(count, SPAN, hk, hd)
    tgt = targets.reshape(count, SPAN, hk, group, hd)
    q_up, q_low, feat_q = hedgehog(q_heads, q_map, "ncxd,xde->ncxe")
    k_up, k_low, feat_k = hedgehog(k_heads, k_map, "ncxd,xde->ncxe")
    feat_q = feat_q.reshape(count, SPAN, hk, group, 2 * hd)
    first = lax.axis_index(SEQ) * count
    lengths = doc_spans[0]
    starts = jnp.cumsum(lengths) - lengths
    ends = starts + lengths
    span_ids = first + jnp.arange(count, dtype=jnp.int32)
    inside = (span_ids[:, None] >= starts[None, :]) & (span_ids[:, None] < ends[None, :])
    span_start = jnp.sum(jnp.where(inside, starts[None, :], 0), axis=1)
    span_end = jnp.sum(jnp.where(inside, ends[None, :], 0), axis=1)
    same = span_start[:, None] == span_start[None, :]
    order = jnp.arange(count, dtype=jnp.int32)
    before = (same & (order[None, :] < order[:, None])).astype(jnp.float32)
    after = (same & (order[None, :] > order[:, None])).astype(jnp.float32)
    carried_in = (span_start < first).astype(jnp.float32)
    carried_out = (span_end > first + count).astype(jnp.float32)
    fresh = jnp.max((span_start >= first).astype(jnp.float32))
    tail = (span_start == span_start[count - 1]).astype(jnp.float32)
    key_state = jnp.einsum("ncxf,ncxd->nxfd", feat_k, vals, preferred_element_type=jnp.float32)
    key_norm = jnp.sum(feat_k.astype(jnp.float32), axis=1)
    zero_state = jnp.zeros(key_state.shape[1:], jnp.float32)
    zero_norm = jnp.zeros(key_norm.shape[1:], jnp.float32)
    nothing = jnp.zeros((), jnp.float32)
    summary = (
        spread_blocks(tail[None, :], key_state)[0],
        spread_blocks(tail[None, :], key_norm)[0],
        fresh,
    )
    state_in, norm_in, _ = carried_in_2(
        summary, SEQ, reset_join, (zero_state, zero_norm, nothing), False
    )
    state = spread_blocks(before, key_state) + carried_in[:, None, None, None] * state_in[None]
    norm = spread_blocks(before, key_norm) + carried_in[:, None, None] * norm_in[None]
    pairs, d_feat_q, back_state, back_norm = span_middle(
        feat_q, feat_k, vals, tgt, state.astype(jnp.bfloat16), norm.astype(jnp.bfloat16), coef
    )
    back_summary = (
        spread_blocks(carried_in[None, :], back_state)[0],
        spread_blocks(carried_in[None, :], back_norm)[0],
        fresh,
    )
    rstate_in, rnorm_in, _ = carried_in_2(
        back_summary, SEQ, reset_join, (zero_state, zero_norm, nothing), True
    )
    rstate = spread_blocks(after, back_state) + carried_out[:, None, None, None] * rstate_in[None]
    rnorm = spread_blocks(after, back_norm) + carried_out[:, None, None] * rnorm_in[None]
    d_feat_k = span_last(
        pairs, feat_q, vals, rstate.astype(jnp.bfloat16), rnorm.astype(jnp.bfloat16)
    )
    du_q = map_grad(q_up, q_low, d_feat_q.reshape(count, SPAN, hq, 2 * hd), hd)
    du_k = map_grad(k_up, k_low, d_feat_k, hd)
    grad_q = jnp.einsum("ncxd,ncxe->xde", q_heads, du_q, preferred_element_type=jnp.float32)
    grad_k = jnp.einsum("ncxd,ncxe->xde", k_heads, du_k, preferred_element_type=jnp.float32)
    flat = jnp.concatenate([grad_q.reshape(-1), grad_k.reshape(-1)])
    share = sum_at_owner(flat, SEQ, 0)
    share = gathered_total(share, "dp")
    whole = gather_directly(share, SEQ, 0)
    split_at = hq * hd * hd
    grad_q = whole[:split_at].reshape(hq, hd, hd)
    grad_k = whole[split_at:].reshape(hk, hd, hd)
    return (grad_q, grad_k)


def solution(mesh):
    split = Mesh(mesh.devices.reshape(mesh.shape["dp"], 4, 8), ("dp", "seq_0", "seq_1"))
    placed = (
        P("dp", SEQ, None),
        P("dp", SEQ, None),
        P("dp", SEQ, None),
        P("dp", SEQ, None),
        P(),
        P(),
        P("dp", None),
    )
    return jax.shard_map(shards, mesh=split, in_specs=placed, out_specs=(P(), P()), check_vma=False)
```

profile of v0, /device:TPU:1, one launch (start us, length us, event | category | flops | bytes accessed | tf_op | source)
XLA Modules:
  0.0 452.3 jit_solution(7657818797668206918)
XLA Ops:
  7.2 1.1 reshape.124
  8.3 1.4 fusion.182
  9.7 1.4 fusion.187
  11.2 0.9 reduce-window.4
  12.8 0.7 select_reduce_fusion
  14.0 1.0 reshape.125
  15.2 1.0 fusion.177
  16.5 3.9 fusion.68
  21.0 0.7 fusion.170
  21.7 1.3 dynamic-update-slice
  23.0 17.4 %all-reduce = f32[8]{0:T(128)S(1)} all-reduce(f32[8]{0:T(128)S(1)} %dynamic-update-slice), channel_id=1, replica_groups=mesh['dp'=8,'seq_0'=4,'seq_1'=8] {'seq_1'}, use_global_device_ids=true, to_apply=%add | all-reduce | flops 8 | bytes 64
  51.2 0.8 dynamic-update-slice.1
  52.0 0.8 dynamic-update-slice.2
  52.8 9.5 %all-reduce.3 = (f32[4]{0:T(128)S(1)}, f32[4]{0:T(128)S(1)}) all-reduce(f32[4]{0:T(128)S(1)} %dynamic-update-slice.1, f32[4]{0:T(128)S(1)} %dynamic-update-slice.2), channel_id=1, replica_groups=mesh['dp'=8,'seq_0'=4,'seq_1'=8] {'seq_0'}, use_global_device_ids=true, to_apply=%add.1 | all-reduce | flops 8 | bytes 64
  67.0 0.7 fusion.179
  70.4 0.8 fusion.161
  71.2 2.1 copy.292
  73.7 2.7 copy.293
  76.4 5.3 %copy.210 = f32[2,128,4,8,128]{1,4,3,2,0:T(8,128)} copy(f32[2,128,4,8,128]{4,3,2,1,0:T(8,128)} %bitcast.415) | data formatting | bytes 8388608 | tf_op jit(solution)/shard_map/convert_element_type | solution.py:97
  81.8 3.3 fusion.35
  85.1 3.2 fusion.90
  88.6 7.7 %fusion.192 = (bf16[2,128,32,128]{1,3,0,2:T(8,128)(2,1)}, f32[2,128,32,128]{1,3,0,2:T(8,128)}) fusion(f32[32,128,2,128]{3,1,2,0:T(8,128)} %fusion.35), kind=kOutput, calls=%fused_computation.261 | output fusion | flops 5259518 | bytes 10485760 | tf_op jit(solution)/shard_map/div | solution.py:69
  96.3 4.0 copy.201
  100.3 7.9 %fusion.193 = (bf16[2,128,32,128]{1,3,0,2:T(8,128)(2,1)}, f32[2,128,32,128]{1,3,0,2:T(8,128)}) fusion(f32[32,128,2,128]{3,1,2,0:T(8,128)} %fusion.35), kind=kOutput, calls=%fused_computation.262 | output fusion | flops 3162366 | bytes 10485760 | tf_op jit(solution)/shard_map/div | solution.py:68
  108.1 4.0 copy.200
  112.1 19.6 %all-gather.5 = f32[8,4,256]{2,1,0:T(4,128)S(1)} all-gather(f32[1,4,256]{2,1,0:T(4,128)S(1)} %copy.245), channel_id=3, replica_groups=mesh['dp'=8,'seq_0'=4,'seq_1'=8] {'seq_1'}, dimensions={0}, use_global_device_ids=true | all-gather | bytes 36864 | tf_op jit(solution)/shard_map/all_gather | solution.py:24
  131.7 9.1 %all_gather.61 = f32[4,4,256]{2,1,0:T(4,128)S(1)} all-gather(f32[1,4,256]{2,1,0:T(4,128)S(1)} %slice_add_fusion.39), channel_id=1, replica_groups=mesh['dp'=8,'seq_0'=4,'seq_1'=8] {'seq_0'}, dimensions={0}, use_global_device_ids=true | all-gather | bytes 20480 | tf_op jit(solution)/shard_map/all_gather | solution.py:24
  141.2 3.4 fusion.131
  144.6 2.7 fusion.20
  147.3 3.5 fusion.70
  150.8 3.6 fusion.85
  155.3 1.5 fusion.178
  157.5 0.7 copy-done.40
  158.2 1.9 multiply_reduce_fusion.3
  160.1 1.4 convolution_bitcast_fusion
  161.6 3.3 fusion.65
  168.3 2.9 multiply_reduce_fusion
  171.8 1.4 fusion.14
  173.2 1.3 copy-done.17
  174.6 1.3 fusion.108
  175.9 4.3 fusion.10
  180.1 8.7 %copy.220 = f32[2,128,4,8,256]{1,4,0,3,2:T(8,128)} copy(f32[2,128,4,8,256]{4,1,3,2,0:T(8,128)} %fusion.10) | data formatting | bytes 16777216 | tf_op jit(solution)/shard_map/add | solution.py:107
  188.8 39.8 %all-gather.18.cloned.1.call-done = f32[32,256,128]{2,1,0:T(8,128)} async-done(((f32[4,256,128]{2,1,0:T(8,128)}), f32[32,256,128]{2,1,0:T(8,128)}) %all-gather.18.cloned.1.call-update) | async-done | bytes 4194320 | tf_op jit(solution)/shard_map/all_gather | solution.py:24
  228.6 3.2 fusion.81
  231.9 6.2 %fusion.2 = f32[2,128,32,128]{1,3,0,2:T(8,128)} fusion(f32[2,128,32,128]{1,3,0,2:T(8,128)} %get-tuple-element.31, f32[2,128,32,256]{1,3,0,2:T(8,128)} %bitcast.410), kind=kOutput, calls=%fused_computation.2 | output fusion | flops 1056895 | bytes 12582912 | tf_op jit(solution)/shard_map/sub | solution.py:77
  238.1 1.2 copy-done.2
  239.2 1.2 copy-done.8
  240.4 2.4 fusion.3
  242.8 12.3 %fusion.37 = f32[32,128,128]{1,2,0:T(8,128)} fusion(bf16[2,128,32,128]{3,2,1,0:T(8,128)(2,1)S(1)} %bitcast.414, f32[2,128,32,128]{1,3,0,2:T(8,128)} %get-tuple-element.31, f32[2,128,32,128]{1,3,0,2:T(8,128)} %fusion.2, f32[2,128,32,128]{1,3,0,2:T(8,128)} %get-tuple-element.33, f32[2,128,32,128]{1,3,0,2:T(8,128)} %fusion.3, f32[2,128,32,256]{1,3,0,2:T(8,128)} %bitcast.411), kind=kOutput, calls=%fused_computation.52 | convolution fusion | flops 274726912 | bytes 29360128 | tf_op jit(solution)/shard_map/ncxd,ncxe->xde/dot_general | solution.py:200
  255.1 3.1 copy.222
  258.2 19.1 %all-gather.6 = f32[8,4,256]{2,1,0:T(4,128)S(1)} all-gather(f32[1,4,256]{2,1,0:T(4,128)S(1)} %copy.270), channel_id=5, replica_groups=mesh['dp'=8,'seq_0'=4,'seq_1'=8] {'seq_1'}, dimensions={0}, use_global_device_ids=true | all-gather | bytes 36864 | tf_op jit(solution)/shard_map/all_gather | solution.py:24
  277.3 9.4 %all_gather.67 = f32[4,4,256]{2,1,0:T(4,128)S(1)} all-gather(f32[1,4,256]{2,1,0:T(4,128)S(1)} %slice_add_fusion.27), channel_id=1, replica_groups=mesh['dp'=8,'seq_0'=4,'seq_1'=8] {'seq_0'}, dimensions={0}, use_global_device_ids=true | all-gather | bytes 20480 | tf_op jit(solution)/shard_map/all_gather | solution.py:24
  287.0 3.3 fusion.40
  290.3 3.5 fusion.76
  293.9 2.9 fusion.47
  297.7 1.5 fusion.59
  299.4 1.7 pad_maximum_fusion.1
  301.2 52.6 %all_to_all.16 = f32[32,1,18432]{2,1,0:T(1,128)} all-to-all(f32[32,1,18432]{2,1,0:T(1,128)S(1)} %bitcast.416), channel_id=1, replica_groups=mesh['dp'=8,'seq_0'=4,'seq_1'=8] {'seq_0','seq_1'}, dimensions={0} | all-to-all | bytes 4718592 | tf_op jit(solution)/shard_map/all_to_all | solution.py:41
  353.8 3.0 reduce_sum.158
  356.8 25.6 %all-gather.4 = f32[147456]{0:T(1024)S(1)} all-gather(f32[18432]{0:T(1024)S(1)} %reduce_sum.158), channel_id=6, replica_groups=mesh['dp'=8,'seq_0'=4,'seq_1'=8] {'dp'}, dimensions={0}, use_global_device_ids=true | all-gather | bytes 663552 | tf_op jit(solution)/shard_map/all_gather | solution.py:46
  382.6 1.2 broadcast_in_dim.51
  383.8 59.3 %all_to_all.15 = f32[32,1,18432]{2,1,0:T(1,128)S(1)} all-to-all(f32[32,1,18432]{2,1,0:T(1,128)S(1)} %broadcast_in_dim.51), channel_id=1, replica_groups=mesh['dp'=8,'seq_0'=4,'seq_1'=8] {'seq_0','seq_1'}, dimensions={0} | all-to-all | bytes 4718592 | tf_op jit(solution)/shard_map/all_to_all | solution.py:52
  443.2 0.7 slice.398
  443.9 1.5 slice.397
  (124 shorter events, 9.5 us)
Async XLA Ops:
  7.2 74.6 %copy-start = (bf16[32,128,128]{2,1,0:T(8,128)(2,1)S(1)}, bf16[32,128,128]{2,1,0:T(8,128)(2,1)}, u32[]{:S(2)}) copy-start(bf16[32,128,128]{2,1,0:T(8,128)(2,1)} %param.11) | copy-start | bytes 3145732
  7.2 77.9 %all-gather.16.cloned.1.call-start = ((), (), s32[]{:S(2)}) async-start(), calls=%async_computation.4 | async-start | bytes 4718592 | tf_op jit(solution)/shard_map/all_gather | solution.py:24
  8.3 7.9 %copy-start.20 = (bf16[2,128,4,128]{3,2,1,0:T(4,128)(2,1)}, bf16[2,128,4,128]{3,2,1,0:T(4,128)(2,1)S(1)}, u32[]{:S(2)}) copy-start(bf16[2,128,4,128]{3,2,1,0:T(4,128)(2,1)S(1)} %reshape.124) | copy-start | bytes 786436
  9.7 6.5 %copy-start.22 = (f32[2,128,4,128]{1,3,0,2:T(8,128)}, f32[2,128,4,128]{1,3,0,2:T(8,128)S(1)}, u32[]{:S(2)}) copy-start(f32[2,128,4,128]{1,3,0,2:T(8,128)S(1)} %get-tuple-element.27) | copy-start | bytes 1572868
  9.7 10.7 %copy-start.30 = (f32[2,128,4]{1,0,2:T(2,128)}, f32[2,128,4]{1,0,2:T(2,128)S(1)}, u32[]{:S(2)}) copy-start(f32[2,128,4]{1,0,2:T(2,128)S(1)} %get-tuple-element.26) | copy-start | bytes 12292
  11.2 59.2 %copy-start.16 = (f32[2,128,4,128]{1,3,0,2:T(8,128)}, f32[2,128,4,128]{1,3,0,2:T(8,128)S(1)}, u32[]{:S(2)}) copy-start(f32[2,128,4,128]{1,3,0,2:T(8,128)S(1)} %get-tuple-element.29) | copy-start | bytes 1572868
  11.2 9.3 %copy-start.36 = (u32[256]{0:T(256)S(1)}, u32[256]{0:T(256)}, u32[]{:S(2)}) copy-start(u32[256]{0:T(256)} %constant.63) | copy-start | bytes 3076
  11.2 29.3 %copy-start.35 = (u32[256]{0:T(256)S(1)}, u32[256]{0:T(256)}, u32[]{:S(2)}) copy-start(u32[256]{0:T(256)} %constant.68) | copy-start | bytes 3076
  13.5 157.7 %copy-start.28 = (s32[2]{0:T(128)}, s32[2]{0:T(128)S(1)}, u32[]{:S(2)}) copy-start(s32[2]{0:T(128)S(1)} %get-tuple-element.3) | copy-start | bytes 28
  16.5 54.7 %copy-start.10 = (f32[2,4,256,128]{3,2,1,0:T(8,128)}, f32[2,4,256,128]{3,2,1,0:T(8,128)S(1)}, u32[]{:S(2)}) copy-start(f32[2,4,256,128]{3,2,1,0:T(8,128)S(1)} %fusion.100) | copy-start | bytes 3145732
  20.4 130.4 %all-gather.12.cloned.1.call-start = ((), (), s32[]{:S(2)}) async-start(), calls=%async_computation.2 | async-start | bytes 2621440 | tf_op jit(solution)/shard_map/all_gather | solution.py:24
  67.0 6.2 %copy-start.13 = (bf16[1,256,4096]{2,1,0:T(8,128)(2,1)S(1)}, bf16[1,256,4096]{2,1,0:T(8,128)(2,1)}, u32[]{:S(2)}) copy-start(bf16[1,256,4096]{2,1,0:T(8,128)(2,1)} %param.10) | copy-start | bytes 6291460
  88.3 140.3 %all-gather.18.cloned.1.call-start = ((), (), s32[]{:S(2)}) async-start(), calls=%async_computation.5 | async-start | bytes 4718592 | tf_op jit(solution)/shard_map/all_gather | solution.py:24
  112.1 32.5 %copy-start.3 = (bf16[2,128,4,8,128]{4,1,3,2,0:T(8,128)(2,1)S(1)}, bf16[2,128,4,8,128]{4,1,3,2,0:T(8,128)(2,1)}, u32[]{:S(2)}) copy-start(bf16[2,128,4,8,128]{4,1,3,2,0:T(8,128)(2,1)} %copy.201) | copy-start | bytes 6291460
  112.1 32.5 %copy-start.6 = (bf16[2,128,4,8,128]{4,1,3,2,0:T(8,128)(2,1)S(1)}, bf16[2,128,4,8,128]{4,1,3,2,0:T(8,128)(2,1)}, u32[]{:S(2)}) copy-start(bf16[2,128,4,8,128]{4,1,3,2,0:T(8,128)(2,1)} %copy.200) | copy-start | bytes 6291460
  112.1 32.5 %copy-start.18 = (bf16[2,128,4,256,1]{1,3,0,2,4:T(8,128)(2,1)S(1)}, bf16[2,128,4,256,1]{1,3,0,2,4:T(8,128)(2,1)}, u32[]{:S(2)}) copy-start(bf16[2,128,4,256,1]{1,3,0,2,4:T(8,128)(2,1)} %get-tuple-element.8) | copy-start | bytes 1572868
  140.9 6.4 %copy-start.24 = (pred[128,128]{0,1:T(8,128)(4,1)}, pred[128,128]{0,1:T(8,128)(4,1)S(1)}, u32[]{:S(2)}) copy-start(pred[128,128]{0,1:T(8,128)(4,1)S(1)} %iota_compare_fusion) | copy-start | bytes 49156
  141.2 6.1 %copy-start.32 = (bf16[2,4,256]{2,0,1:T(2,128)(2,1)}, bf16[2,4,256]{2,0,1:T(2,128)(2,1)S(1)}, u32[]{:S(2)}) copy-start(bf16[2,4,256]{2,0,1:T(2,128)(2,1)S(1)} %fusion.60) | copy-start | bytes 12292
  144.6 2.7 copy-start.11
  150.8 3.6 copy-start.12
  150.8 3.8 copy-start.4
  150.8 4.4 copy-start.7
  155.3 2.2 copy-start.9
  155.3 2.2 copy-start.25
  155.3 2.9 copy-start.40
  160.1 1.5 copy-start.14
  160.1 5.1 %copy-start.33 = (bf16[2,4,256]{2,0,1:T(2,128)(2,1)S(1)}, bf16[2,4,256]{2,0,1:T(2,128)(2,1)}, u32[]{:S(2)}) copy-start(bf16[2,4,256]{2,0,1:T(2,128)(2,1)} %copy-done.32) | copy-start | bytes 12292
  160.1 7.6 %copy-start.34 = (s32[2]{0:T(128)S(1)}, s32[2]{0:T(128)}, u32[]{:S(2)}) copy-start(s32[2]{0:T(128)} %get-tuple-element.2) | copy-start | bytes 28
  161.6 3.3 copy-start.38
  164.9 125.4 %all-gather.14.cloned.1.call-start = ((), (), s32[]{:S(2)}) async-start(), calls=%async_computation.3 | async-start | bytes 2621440 | tf_op jit(solution)/shard_map/all_gather | solution.py:24
  165.3 6.5 %copy-start.15 = (bf16[2,128,4,8,128]{1,4,3,2,0:T(8,128)(2,1)S(1)}, bf16[2,128,4,8,128]{1,4,3,2,0:T(8,128)(2,1)}, u32[]{:S(2)}) copy-start(bf16[2,128,4,8,128]{1,4,3,2,0:T(8,128)(2,1)} %copy-done.14) | copy-start | bytes 6291460
  168.3 6.3 %copy-start.19 = (bf16[2,128,4,256,1]{1,3,0,2,4:T(8,128)(2,1)S(1)}, bf16[2,128,4,256,1]{1,3,0,2,4:T(8,128)(2,1)}, u32[]{:S(2)}) copy-start(bf16[2,128,4,256,1]{1,3,0,2,4:T(8,128)(2,1)} %get-tuple-element.8) | copy-start | bytes 1572868
  171.2 0.6 copy-start.26
  173.2 1.3 copy-start.17
  231.9 7.4 %copy-start.2 = (f32[2,128,4,8,256]{1,4,0,3,2:T(8,128)S(1)}, f32[2,128,4,8,256]{1,4,0,3,2:T(8,128)}, u32[]{:S(2)}) copy-start(f32[2,128,4,8,256]{1,4,0,3,2:T(8,128)} %copy.220) | copy-start | bytes 25165828
  231.9 8.5 %copy-start.8 = (f32[2,128,32,128]{1,3,0,2:T(8,128)S(1)}, f32[2,128,32,128]{1,3,0,2:T(8,128)}, u32[]{:S(2)}) copy-start(f32[2,128,32,128]{1,3,0,2:T(8,128)} %get-tuple-element.33) | copy-start | bytes 12582916
  255.1 31.6 %copy-start.27 = (f32[2,4,256]{2,1,0:T(4,128)S(1)}, f32[2,4,256]{2,1,0:T(4,128)}, u32[]{:S(2)}) copy-start(f32[2,4,256]{2,1,0:T(4,128)} %copy-done.26) | copy-start | bytes 24580
  255.1 31.7 %copy-start.29 = (s32[2]{0:T(128)S(1)}, s32[2]{0:T(128)}, u32[]{:S(2)}) copy-start(s32[2]{0:T(128)} %copy-done.28) | copy-start | bytes 28
  255.1 31.7 %copy-start.37 = (f32[2]{0:T(128)S(1)}, f32[2]{0:T(128)}, u32[]{:S(2)}) copy-start(f32[2]{0:T(128)} %compare_convert_fusion) | copy-start | bytes 28
  255.1 31.9 %copy-start.5 = (bf16[2,128,4,8,128]{4,1,3,2,0:T(8,128)(2,1)S(1)}, bf16[2,128,4,8,128]{4,1,3,2,0:T(8,128)(2,1)}, u32[]{:S(2)}) copy-start(bf16[2,128,4,8,128]{4,1,3,2,0:T(8,128)(2,1)} %copy.201) | copy-start | bytes 6291460
  290.3 3.5 copy-start.39
  293.9 3.5 copy-start.23
  293.9 3.5 copy-start.31
  296.8 1.0 copy-start.21
  382.6 62.8 %copy-start.1 = (bf16[32,128,128]{2,1,0:T(8,128)(2,1)S(1)}, bf16[32,128,128]{2,1,0:T(8,128)(2,1)}, u32[]{:S(2)}) copy-start(bf16[32,128,128]{2,1,0:T(8,128)(2,1)} %param.11) | copy-start | bytes 3145732
Sparse Core Ops, SparseCore 0:
  20.5 58.5 all-gather.15
  88.5 33.7 all-gather.11
  165.0 63.5 all-gather.17
  232.0 31.9 all-gather.13
where the time goes:
time: 461 us; the launch traced here: 452 us
  blocking collectives  222 us (48%)
  matrix products  56.9 us (12%)
  other arithmetic  51.4 us (11%)
  local copies, waits for them, and re-layouts  47.9 us (10%)
  waiting for transfers between devices  39.9 us (9%)
  between operations  33.9 us (7%)
    all_to_all x1, blocking collectives, sent_to_all(): return lax.all_to_all(copies, axis, split_axis=0, concat_axis=0, tiled=True)  59.3 us
    all_gather x4, blocking collectives, carried_in_2(): pieces = jax.tree.map(lambda part: lax.all_gather(part, axis), total)  57.2 us
    all_to_all x1, blocking collectives, sum_at_owner(): lax.all_to_all(blocks, axis, split_axis=0, concat_axis=0, tiled=True)  52.6 us
    all_gather x4, waiting for transfers between devices, carried_in_2(): pieces = jax.tree.map(lambda part: lax.all_gather(part, axis), total)  39.8 us
    unnamed x2, blocking collectives  27 us
    all_gather x1, blocking collectives, gathered_total(): blocks = lax.all_gather(shard, axis)  25.6 us
    unnamed x92, local copies, waits for them, and re-layouts  15.2 us
    dot_general x8, matrix products, spread_blocks(): jnp.einsum('cy,y...->c...', weights, blocks, precision=lax.Precision.HIGH...  14.9 us
  transfers between devices with their start and end apart: 4, of which 1 were waited for; matrix products, arithmetic and copies ran while one was open for 22% of the time, Pallas kernels for 0%

commit v1 on v0

v1 whole, which is shorter than its diff:
```python
import functools
import math

import jax
import jax.numpy as jnp
from jax import lax
from jax.experimental import pallas as pl
from jax.experimental.pallas import tpu as pltpu
from jax.sharding import PartitionSpec as P

MESH = pl.DeviceIdType.MESH
F32 = jnp.float32
BF16 = jnp.bfloat16
SPAN = 128
HD = 128
HK = 4
GROUP = 8
NDOC = 8
NZ = 8
NY = 4
NDP = 8
SLICE = 136
ROWS = NZ * SLICE
ZROW = HK * 256


def dot(a, b, ca, cb):
    return lax.dot_general(a, b, (((ca,), (cb,)), ((), ())), preferred_element_type=F32)


def starts_of(spans_ref):
    starts, total = [], jnp.int32(0)
    for n in range(NDOC):
        starts.append(total)
        total = total + spans_ref[0, n]
    return starts


def no_start(starts, *blocks):
    hit = jnp.bool_(False)
    for s in starts:
        for b in blocks:
            hit = jnp.logical_or(hit, s == b)
    return jnp.where(hit, 0.0, 1.0).astype(F32)


def softmax_pair(u):
    e1 = jnp.exp(u - jnp.max(u, -1, keepdims=True))
    e2 = jnp.exp(jnp.min(u, -1, keepdims=True) - u)
    p1 = e1 * (1.0 / jnp.sum(e1, -1, keepdims=True))
    p2 = e2 * (1.0 / jnp.sum(e2, -1, keepdims=True))
    return p1, p2


def map_grad(p1, p2, d1, d2):
    s1 = jnp.sum(p1 * d1, -1, keepdims=True)
    s2 = jnp.sum(p2 * d2, -1, keepdims=True)
    return (p1 * (d1 - s1) - p2 * (d2 - s2)).astype(BF16)


def key_kernel(spans_ref, k_ref, v_ref, w_ref, fk_ref, pk_ref, st0_ref, sum_ref, co_ref):
    seq = lax.axis_index("seq")
    y = seq // NZ
    starts = starts_of(spans_ref)
    same = no_start(starts, 2 * seq + 1)
    st0_ref[pl.ds(ZROW, ROWS - ZROW), :] = jnp.zeros((ROWS - ZROW, 128), F32)
    sum_ref[pl.ds(ZROW, ROWS - ZROW), :] = jnp.zeros((ROWS - ZROW, 128), F32)
    for h in range(HK):
        cols = slice(h * HD, (h + 1) * HD)
        u = dot(k_ref[:, cols], w_ref[h], 1, 0)
        p1, p2 = softmax_pair(u)
        pk_ref[0, :, cols] = p1
        pk_ref[1, :, cols] = p2
        fk = jnp.concatenate([p1, p2], -1).astype(BF16)
        fk_ref[:, h * 256 : (h + 1) * 256] = fk
        v = v_ref[:, cols]
        st = [dot(v[c * SPAN : (c + 1) * SPAN], fk[c * SPAN : (c + 1) * SPAN], 0, 0) for c in (0, 1)]
        zs = [jnp.sum(fk[c * SPAN : (c + 1) * SPAN].astype(F32), 0, keepdims=True) for c in (0, 1)]
        for half in (0, 1):
            part = slice(half * 128, (half + 1) * 128)
            rows = pl.ds(h * 256 + half * 128, 128)
            st0_ref[rows, :] = st[0][:, part]
            sum_ref[rows, :] = same * st[0][:, part] + st[1][:, part]
            zr = pl.ds(ZROW + 2 * h + half, 1)
            st0_ref[zr, :] = zs[0][:, part]
            sum_ref[zr, :] = same * zs[0][:, part] + zs[1][:, part]
    pos = lax.broadcasted_iota(jnp.int32, (NZ, 128), 0) + y * NZ
    hit = jnp.zeros((NZ, 128), F32)
    for s in starts:
        hit = jnp.where(pos == s // 2, 1.0, hit)
    co_ref[0:8, :] = 1.0 - hit
    last = jnp.float32(1.0)
    nxt = jnp.float32(1.0)
    for s in starts:
        last = jnp.where(s // 16 == y - 1, 0.0, last)
        nxt = jnp.where(s // 16 == y + 1, 0.0, nxt)
    co_ref[8:9, :] = jnp.full((1, 128), jnp.where(y >= 1, 1.0, 0.0), F32)
    co_ref[9:10, :] = jnp.full((1, 128), jnp.where(y >= 2, last, 0.0), F32)
    co_ref[10:11, :] = jnp.full((1, 128), jnp.where(y <= 2, 1.0, 0.0), F32)
    co_ref[11:12, :] = jnp.full((1, 128), jnp.where(y <= 1, nxt, 0.0), F32)
    co_ref[12:16, :] = jnp.zeros((4, 128), F32)


def remote(src, dst, send, recv, dev):
    return pltpu.make_async_remote_copy(
        src_ref=src, dst_ref=dst, send_sem=send, recv_sem=recv, device_id=dev, device_id_type=MESH
    )


def rows_of(index, size):
    return pl.ds(pl.multiple_of(index * size, 8), size)


def where_am_i():
    dp = lax.axis_index("dp")
    seq = lax.axis_index("seq")
    return dp, seq, lax.div(seq, NZ), lax.rem(seq, NZ)


def greet(peers):
    barrier = pltpu.get_barrier_semaphore()
    for dev in peers:
        pl.semaphore_signal(barrier, inc=1, device_id=dev, device_id_type=MESH)
    pl.semaphore_wait(barrier, len(peers))


def z_peers(dp, y, z):
    return [(dp, y * NZ + lax.rem(z + d, NZ)) for d in range(1, NZ)]


def y_peers(dp, y, z):
    return [(dp, lax.rem(y + d, NY) * NZ + z) for d in range(1, NY)]


def scan_scratch():
    return [
        pltpu.VMEM((NZ, SLICE, 128), F32),
        pltpu.VMEM((SLICE, 128), F32),
        pltpu.VMEM((2, SLICE, 128), F32),
        pltpu.VMEM((NZ, SLICE, 128), F32),
        pltpu.SemaphoreType.DMA((2, NZ)),
        pltpu.SemaphoreType.DMA((2, 2)),
        pltpu.SemaphoreType.DMA((2, NZ)),
    ]


class Scan:
    def __init__(self, own, out, co, scratch, reverse):
        self.own, self.out, self.co, self.reverse = own, out, co, reverse
        self.seen, self.total, self.rows_in, self.back, self.s1, self.s2, self.s3 = scratch
        self.dp, self.seq, self.y, self.z = where_am_i()

    def start(self):
        self.copies = []
        for d in range(1, NZ):
            to = lax.rem(self.z + d, NZ)
            copy = remote(
                self.own.at[rows_of(to, SLICE)],
                self.seen.at[self.z],
                self.s1.at[0, d],
                self.s1.at[1, d],
                (self.dp, self.y * NZ + to),
            )
            copy.start()
            self.copies.append(copy)

    def totals(self):
        self.seen[self.z] = self.own[rows_of(self.z, SLICE), :]
        for copy in self.copies:
            copy.wait_recv()
        order = list(range(NZ))[::-1] if self.reverse else list(range(NZ))
        acc = jnp.zeros((SLICE, 128), F32)
        for k in order:
            self.back[k] = acc
            acc = self.seen[k] + self.co[k : k + 1, :] * acc
        self.total[...] = acc
        self.row_copies = []
        for d in (1, 2):
            step = NY - d if self.reverse else d
            copy = remote(
                self.total,
                self.rows_in.at[d - 1],
                self.s2.at[0, d - 1],
                self.s2.at[1, d - 1],
                (self.dp, lax.rem(self.y + step, NY) * NZ + self.z),
            )
            copy.start()
            self.row_copies.append(copy)

    def give_back(self):
        for copy in self.row_copies:
            copy.wait_recv()
        first = 10 if self.reverse else 8
        carry = (
            self.co[first : first + 1, :] * self.rows_in[0]
            + self.co[first + 1 : first + 2, :] * self.rows_in[1]
        )
        order = list(range(NZ))[::-1] if self.reverse else list(range(NZ))
        keep = jnp.ones((1, 128), F32)
        for k in order:
            self.back[k] = self.back[k] + keep * carry
            keep = keep * self.co[k : k + 1, :]
        self.out[rows_of(self.z, SLICE), :] = self.back[self.z]
        self.back_copies = []
        for d in range(1, NZ):
            to = lax.rem(self.z + d, NZ)
            copy = remote(
                self.back.at[to],
                self.out.at[rows_of(self.z, SLICE)],
                self.s3.at[0, d],
                self.s3.at[1, d],
                (self.dp, self.y * NZ + to),
            )
            copy.start()
            self.back_copies.append(copy)

    def arrived(self):
        for copy in self.back_copies:
            copy.wait_recv()

    def finish(self):
        for copy in self.copies + self.row_copies + self.back_copies:
            copy.wait_send()


def state_kernel(own_ref, co_ref, out_ref, *scratch):
    dp, seq, y, z = where_am_i()
    greet(z_peers(dp, y, z) + y_peers(dp, y, z))
    scan = Scan(own_ref, out_ref, co_ref, scratch, False)
    scan.start()
    scan.totals()
    scan.give_back()
    scan.arrived()
    scan.finish()


def middle_kernel(
    coef, spans_ref, q_ref, t_ref, v_ref, fk_ref, w_ref, st0_ref, st0z_ref, in_ref, inz_ref,
    gq_ref, back_ref, back1_ref, dfk_ref, fq_s, x_s, p_s, m_s,
):
    head = pl.program_id(0)
    block = pl.program_id(1)
    seq = lax.axis_index("seq")
    starts = starts_of(spans_ref)
    b0 = 2 * seq
    in0 = no_start(starts, b0)
    same = no_start(starts, b0 + 1)
    in1 = no_start(starts, b0, b0 + 1)
    w_in = jnp.where(block == 0, in0, in1)
    w_st = jnp.where(block == 0, 0.0, same)
    m_s[0:128, :] = fk_ref[...]
    zb = []
    for half in (0, 1):
        rows = slice(half * 128, (half + 1) * 128)
        m_s[128:256, rows] = (w_in * in_ref[rows, :] + w_st * st0_ref[rows, :]).astype(BF16)
        zr = pl.ds(2 * head + half, 1)
        zb.append((w_in * inz_ref[zr, :] + w_st * st0z_ref[zr, :]).astype(BF16).astype(F32))
    m = m_s[...]
    v = v_ref[...]
    causal = lax.broadcasted_iota(jnp.int32, (SPAN, SPAN), 0) >= lax.broadcasted_iota(
        jnp.int32, (SPAN, SPAN), 1
    )
    gz = [jnp.zeros((8, 128), F32), jnp.zeros((8, 128), F32)]
    for g in range(GROUP):
        cols = slice(g * HD, (g + 1) * HD)
        rows = slice(g * SPAN, (g + 1) * SPAN)
        q = q_ref[:, cols]
        p1, p2 = softmax_pair(dot(q, w_ref[g], 1, 0))
        f1 = p1.astype(BF16)
        f2 = p2.astype(BF16)
        fq_s[rows, 0:128] = f1
        fq_s[rows, 128:256] = f2
        p_s[g % 2, 0] = p1
        p_s[g % 2, 1] = p2
        both = dot(fq_s[rows, :], m, 1, 1)
        scores = jnp.where(causal, both[:, 0:128], 0.0)
        f1 = f1.astype(F32)
        f2 = f2.astype(F32)
        den = jnp.sum(scores + f1 * zb[0] + f2 * zb[1], -1, keepdims=True)
        inv = 1.0 / den
        num = dot(scores.astype(BF16), v, 1, 0) + both[:, 128:256]
        out = num * inv
        dy = coef * (out - t_ref[:, cols].astype(F32))
        dnum = (dy * inv).astype(BF16)
        dden = -jnp.sum(dy * out, -1, keepdims=True) * inv
        pairs = jnp.where(causal, dot(dnum, v, 1, 1) + dden, 0.0).astype(BF16)
        x_s[rows, 0:128] = pairs
        x_s[rows, 128:256] = dnum
        for half, f in ((0, f1), (1, f2)):
            gz[half] = gz[half] + jnp.sum((f * dden).reshape(SPAN // 8, 8, 128), 0)
        dfq = dot(x_s[rows, :], m, 1, 0)
        duq = map_grad(
            p_s[g % 2, 0], p_s[g % 2, 1], dfq[:, 0:128] + dden * zb[0], dfq[:, 128:256] + dden * zb[1]
        )
        grad = dot(q, duq, 0, 0)

        @pl.when(block == 0)
        def _():
            gq_ref[g] = grad

        @pl.when(block == 1)
        def _():
            gq_ref[g] = gq_ref[g] + grad

    acc = dot(x_s[...], fq_s[...], 0, 0)
    dfk_ref[...] = acc[0:128, :]

    @pl.when(jnp.logical_and(head == 0, block == 0))
    def _():
        back_ref[pl.ds(ZROW, ROWS - ZROW), :] = jnp.zeros((ROWS - ZROW, 128), F32)
        back1_ref[pl.ds(ZROW, ROWS - ZROW), :] = jnp.zeros((ROWS - ZROW, 128), F32)

    for half in (0, 1):
        part = acc[128:256, half * 128 : (half + 1) * 128]
        zpart = jnp.sum(gz[half], 0, keepdims=True)
        rows = pl.ds(pl.multiple_of(head * 256 + half * 128, 128), 128)
        zr = pl.ds(ZROW + 2 * head + half, 1)

        @pl.when(block == 0)
        def _():
            back_ref[rows, :] = in0 * part
            back_ref[zr, :] = in0 * zpart

        @pl.when(block == 1)
        def _():
            back_ref[rows, :] = back_ref[rows, :] + in1 * part
            back_ref[zr, :] = back_ref[zr, :] + in1 * zpart
            back1_ref[rows, :] = part
            back1_ref[zr, :] = zpart


def send_all(items):
    copies = [remote(*item) for item in items]
    for copy in copies:
        copy.start()
    return copies


def last_kernel(
    spans_ref, own_ref, co_ref, back1_ref, dfk_ref, pk_ref, k_ref, v_ref, gq_ref,
    oq_ref, ok_ref, rin, half_in, half, xy_in, quarter, z_in, gk, kd_in, kd, ky_in, ky, kz_in,
    sc, sxy, sz, az, axy, ac, skd, sky, skz, aky, akd, *scratch,
):
    dp, seq, y, z = where_am_i()
    x, core = lax.div(dp, 2), lax.rem(dp, 2)

    def plane(d):
        px, py = lax.rem(x + d // 4, 4), lax.rem(y + d % 4, 4)
        return px, py, (px * 2 + core, py * NZ + z)

    mate = (x * 2 + (1 - core), seq)
    zs = z_peers(dp, y, z)
    dps = [(lax.rem(dp + d, NDP), seq) for d in range(1, NDP)]
    planes = [plane(d)[2] for d in range(1, 16)]
    other = [(lax.rem(x + d, 4) * 2 + (1 - core), seq) for d in range(4)]
    greet(zs + planes + other)

    scan = Scan(own_ref, rin, co_ref, scratch, True)
    scan.start()
    pair = send_all([(gq_ref.at[rows_of(1 - core, 2048)], half_in, sc.at[0], sc.at[1], mate)])
    pair[0].wait_recv()
    half[...] = gq_ref[rows_of(core, 2048), :] + half_in[...]
    spread = []
    for d in range(1, 16):
        px, py, dev = plane(d)
        spread.append((half.at[rows_of(px * 4 + py, 128)], xy_in.at[d], sxy.at[0, d], sxy.at[1, d], dev))
    spread = send_all(spread)
    scan.totals()
    scan.give_back()
    for copy in spread:
        copy.wait_recv()
    me_xy = x * 4 + y
    acc = half[rows_of(me_xy, 128), :]
    for d in range(1, 16):
        acc = acc + xy_in[d]
    quarter[...] = acc
    base = core * 2048 + me_xy * 128
    zsend = send_all([
        (quarter.at[rows_of(lax.rem(z + d, NZ), 16)], z_in.at[d], sz.at[0, d], sz.at[1, d], zs[d - 1])
        for d in range(1, NZ)
    ])
    scan.arrived()

    starts = starts_of(spans_ref)
    b0 = 2 * seq
    same = no_start(starts, b0 + 1)
    out0 = no_start(starts, b0 + 1, b0 + 2)
    out1 = no_start(starts, b0 + 2)
    for h in range(HK):
        cols = slice(h * HD, (h + 1) * HD)
        total = jnp.zeros((HD, HD), F32)
        for c in (0, 1):
            toks = slice(c * SPAN, (c + 1) * SPAN)
            grads = []
            for hf in (0, 1):
                rows = slice(h * 256 + hf * 128, h * 256 + (hf + 1) * 128)
                zr = slice(ZROW + 2 * h + hf, ZROW + 2 * h + hf + 1)
                if c == 0:
                    r = same * back1_ref[rows, :] + out0 * rin[rows, :]
                    rz = same * back1_ref[zr, :] + out0 * rin[zr, :]
                else:
                    r = out1 * rin[rows, :]
                    rz = out1 * rin[zr, :]
                f = slice(h * 256 + hf * 128, h * 256 + (hf + 1) * 128)
                grads.append(
                    dfk_ref[toks, f] + dot(v_ref[toks, cols], r.astype(BF16), 1, 0)
                    + rz.astype(BF16).astype(F32)
                )
            duk = map_grad(pk_ref[0, toks, cols], pk_ref[1, toks, cols], grads[0], grads[1])
            total = total + dot(k_ref[toks, cols], duk, 0, 0)
        gk[h * HD : (h + 1) * HD, :] = total
    kdsend = send_all([
        (gk.at[rows_of(lax.rem(dp + d, NDP), 64)], kd_in.at[d], skd.at[0, d], skd.at[1, d], dps[d - 1])
        for d in range(1, NDP)
    ])

    for copy in zsend:
        copy.wait_recv()
    acc = quarter[rows_of(z, 16), :]
    for d in range(1, NZ):
        acc = acc + z_in[d]
    mine = pl.ds(pl.multiple_of(base + z * 16, 8), 16)
    oq_ref[mine, :] = acc
    zback = send_all([
        (oq_ref.at[mine], oq_ref.at[mine], az.at[0, d], az.at[1, d], zs[d - 1]) for d in range(1, NZ)
    ])

    for copy in kdsend:
        copy.wait_recv()
    acc = gk[rows_of(dp, 64), :]
    for d in range(1, NDP):
        acc = acc + kd_in[d]
    kd[...] = acc
    ys = y_peers(dp, y, z)
    kysend = send_all([
        (kd.at[rows_of(lax.rem(y + d, NY), 16)], ky_in.at[d], sky.at[0, d], sky.at[1, d], ys[d - 1])
        for d in range(1, NY)
    ])

    for copy in zback:
        copy.wait_recv()
    block = pl.ds(pl.multiple_of(base, 128), 128)
    xyback = send_all([
        (oq_ref.at[block], oq_ref.at[block], axy.at[0, d], axy.at[1, d], planes[d - 1])
        for d in range(1, 16)
    ])

    for copy in kysend:
        copy.wait_recv()
    acc = kd[rows_of(y, 16), :]
    for d in range(1, NY):
        acc = acc + ky_in[d]
    ky[...] = acc
    kz_in[z] = acc
    kzsend = send_all([
        (ky, kz_in.at[z], skz.at[0, d], skz.at[1, d], zs[d - 1]) for d in range(1, NZ)
    ])
    for copy in kzsend:
        copy.wait_recv()
    acc = kz_in[0]
    for k in range(1, NZ):
        acc = acc + kz_in[k]
    kmine = pl.ds(pl.multiple_of(dp * 64 + y * 16, 8), 16)
    ok_ref[kmine, :] = acc
    kyback = send_all([
        (ok_ref.at[kmine], ok_ref.at[kmine], aky.at[0, d], aky.at[1, d], ys[d - 1]) for d in range(1, NY)
    ])
    for copy in kyback:
        copy.wait_recv()
    kblock = rows_of(dp, 64)
    kdback = send_all([
        (ok_ref.at[kblock], ok_ref.at[kblock], akd.at[0, d], akd.at[1, d], dps[d - 1])
        for d in range(1, NDP)
    ])

    for copy in xyback:
        copy.wait_recv()
    whole = rows_of(core, 2048)
    back = send_all([(oq_ref.at[whole], oq_ref.at[whole], ac.at[0], ac.at[1], mate)])
    for copy in kdback + back:
        copy.wait_recv()
    scan.finish()
    for copy in pair + spread + zsend + kdsend + zback + kysend + xyback + kzsend + kyback + kdback + back:
        copy.wait_send()


VM = pl.BlockSpec(memory_space=pltpu.VMEM)
SM = pl.BlockSpec(memory_space=pltpu.SMEM)
LIMIT = 56 * 1024 * 1024


def shape(dims, dtype=F32):
    return jax.ShapeDtypeStruct(dims, dtype)


def shards(queries, keys, values, targets, q_map, k_map, doc_spans):
    q, t = queries[0], targets[0]
    k, v = keys[0], values[0]
    toks = q.shape[0]
    coef = 2.0 / math.sqrt(lax.axis_size("dp") * lax.axis_size("seq") * toks * HD)
    fk, pk, st0, own, co = pl.pallas_call(
        key_kernel,
        out_shape=(
            shape((toks, HK * 256), BF16), shape((2, toks, HK * HD)), shape((ROWS, 128)),
            shape((ROWS, 128)), shape((16, 128)),
        ),
        in_specs=[SM, VM, VM, VM],
        out_specs=(VM,) * 5,
        compiler_params=pltpu.CompilerParams(vmem_limit_bytes=LIMIT),
        name="keys",
    )(doc_spans, k, v, k_map)

    state_in = pl.pallas_call(
        state_kernel,
        out_shape=shape((ROWS, 128)),
        in_specs=[VM, VM],
        out_specs=VM,
        scratch_shapes=scan_scratch(),
        compiler_params=pltpu.CompilerParams(
            collective_id=0, has_side_effects=True, vmem_limit_bytes=LIMIT
        ),
        name="scan",
    )(own, co)

    head_rows = pl.BlockSpec((256, 128), lambda i, c: (i, 0))
    z_rows = pl.BlockSpec((8, 128), lambda i, c: (ZROW // 8, 0))
    whole = pl.BlockSpec((ROWS, 128), lambda i, c: (0, 0))
    gq, back, back1, dfk = pl.pallas_call(
        functools.partial(middle_kernel, coef),
        grid=(HK, 2),
        out_shape=(
            shape((HK * GROUP, HD, HD)), shape((ROWS, 128)), shape((ROWS, 128)), shape((toks, HK * 256)),
        ),
        in_specs=[
            SM,
            pl.BlockSpec((SPAN, GROUP * HD), lambda i, c: (c, i)),
            pl.BlockSpec((SPAN, GROUP * HD), lambda i, c: (c, i)),
            pl.BlockSpec((SPAN, HD), lambda i, c: (c, i)),
            pl.BlockSpec((SPAN, 256), lambda i, c: (c, i)),
            pl.BlockSpec((GROUP, HD, HD), lambda i, c: (i, 0, 0)),
            head_rows, z_rows, head_rows, z_rows,
        ],
        out_specs=(
            pl.BlockSpec((GROUP, HD, HD), lambda i, c: (i, 0, 0)),
            whole, whole,
            pl.BlockSpec((SPAN, 256), lambda i, c: (c, i)),
        ),
        scratch_shapes=[
            pltpu.VMEM((GROUP * SPAN, 256), BF16),
            pltpu.VMEM((GROUP * SPAN, 256), BF16),
            pltpu.VMEM((2, 2, SPAN, 128), F32),
            pltpu.VMEM((256, 256), BF16),
        ],
        compiler_params=pltpu.CompilerParams(
            dimension_semantics=("arbitrary", "arbitrary"), vmem_limit_bytes=LIMIT
        ),
        name="middle",
    )(doc_spans, q, t, v, fk, q_map, st0, st0, state_in, state_in)

    dma = pltpu.SemaphoreType.DMA
    gq, gk = pl.pallas_call(
        last_kernel,
        out_shape=(shape((HK * GROUP * HD, HD)), shape((HK * HD, HD))),
        in_specs=[SM] + [VM] * 8,
        out_specs=(VM, VM),
        scratch_shapes=[
            pltpu.VMEM((ROWS, 128), F32),
            pltpu.VMEM((2048, 128), F32),
            pltpu.VMEM((2048, 128), F32),
            pltpu.VMEM((16, 128, 128), F32),
            pltpu.VMEM((128, 128), F32),
            pltpu.VMEM((NZ, 16, 128), F32),
            pltpu.VMEM((HK * HD, 128), F32),
            pltpu.VMEM((NDP, 64, 128), F32),
            pltpu.VMEM((64, 128), F32),
            pltpu.VMEM((NY, 16, 128), F32),
            pltpu.VMEM((16, 128), F32),
            pltpu.VMEM((NZ, 16, 128), F32),
            dma((2,)), dma((2, 16)), dma((2, NZ)), dma((2, NZ)), dma((2, 16)), dma((2,)),
            dma((2, NDP)), dma((2, NY)), dma((2, NZ)), dma((2, NY)), dma((2, NDP)),
        ] + scan_scratch(),
        compiler_params=pltpu.CompilerParams(
            collective_id=1, has_side_effects=True, vmem_limit_bytes=LIMIT
        ),
        name="last",
    )(doc_spans, back, co, back1, dfk, pk, k, v, gq.reshape(HK * GROUP * HD, HD))
    return gq.reshape(HK * GROUP, HD, HD), gk.reshape(HK, HD, HD)


def solution(mesh):
    placed = (
        P("dp", "seq", None), P("dp", "seq", None), P("dp", "seq", None), P("dp", "seq", None),
        P(), P(), P("dp", None),
    )
    return jax.shard_map(shards, mesh=mesh, in_specs=placed, out_specs=(P(), P()), check_vma=False)
```

time: 461 us -> 199 us (0.43); the launches traced: 452 us -> 198 us
  blocking collectives: 222 us -> 0 us
  Pallas kernels: 0 us -> 193 us
  matrix products: 56.9 us -> 0 us
  other arithmetic: 51.4 us -> 0 us
  local copies, waits for them, and re-layouts: 47.9 us -> 3.88 us
  waiting for transfers between devices: 39.9 us -> 0 us
  between operations: 33.9 us -> 0.66 us
    pallas_call x0 -> x4, Pallas kernels: none -> 193 us  [the longest x1 73.8 us: shards(): pl.pallas_call(last_kernel, out_shape=(shape((HK * GROUP * HD, HD)), shap...]
    all_to_all x2 -> x0, blocking collectives: 112 us -> none  [the longest x1 59.3 us: sent_to_all(): return lax.all_to_all(copies, axis, split_axis=0, concat_axis=0, tiled=True)]
    all_gather x5 -> x0, blocking collectives: 82.8 us -> none  [the longest x4 57.2 us: carried_in_2(): pieces = jax.tree.map(lambda part: lax.all_gather(part, axis), total)]
    dot_general x22 -> x0, matrix products: 54.1 us -> none  [the longest x8 14.9 us: spread_blocks(): jnp.einsum('cy,y...->c...', weights, blocks, precision=lax.Precision.HIGH...]
    all_gather x4 -> x0, waiting for transfers between devices: 39.8 us -> none  [carried_in_2(): pieces = jax.tree.map(lambda part: lax.all_gather(part, axis), total)]
    unnamed x2 -> x0, blocking collectives: 27 us -> none
    div x4 -> x0, other arithmetic: 15.6 us -> none  [the longest x1 7.88 us: hedgehog(): upper = jax.nn.softmax(mapped, axis=-1)]
    unnamed x92 -> x4, local copies, waits for them, and re-layouts: 15.2 us -> 3.88 us
  transfers between devices with their start and end apart: 4 -> 0, of which waited for: 1 -> 0; matrix products, arithmetic and copies ran while one was open for 22% -> 0% of each run, Pallas kernels for 0% -> 0%
where the time goes in v1:
time: 199 us; the launch traced here: 198 us
  Pallas kernels  193 us (97%)
  local copies, waits for them, and re-layouts  3.88 us (2%)
    pallas_call x1, Pallas kernels, shards(): pl.pallas_call(last_kernel, out_shape=(shape((HK * GROUP * HD, HD)), shap...  73.8 us
    pallas_call x1, Pallas kernels, shards(): pl.pallas_call(functools.partial(middle_kernel, coef), grid=(HK, 2), out_...  73.4 us
    pallas_call x1, Pallas kernels, shards(): pl.pallas_call(state_kernel, out_shape=shape((ROWS, 128)), in_specs=[VM,...  42 us
    pallas_call x1, Pallas kernels, shards(): pl.pallas_call(key_kernel, out_shape=(shape((toks, HK * 256), BF16), shap...  4.07 us

profile of v1, /device:TPU:1, one launch (start us, length us, event | category | flops | bytes accessed | tf_op | source)
XLA Modules:
  0.0 197.7 jit_solution(11692102971906108257)
XLA Ops:
  0.6 4.1 %keys.1 = (bf16[256,1024]{1,0:T(8,128)(2,1)}, f32[2,256,512]{2,1,0:T(8,128)}, f32[1088,128]{1,0:T(8,128)}, f32[1088,128]{1,0:T(8,128)}, f32[16,128]{1,0:T(8,128)}) custom-call(s32[1,8]{1,0:T(1,128)} %spans_ref.5, bf16[256,512]{1,0:T(8,128)(2,1)} %bitcast.14, bf16[256,512]{1,0:T(8,128)(2,1)} %bitcast.7, bf16[4,128,128]{2,1,0:T(8,128)(2,1)} %w_ref.2), custom_call_target="tpu_custom_call" | custom-call | tf_op jit(solution)/shard_map/keys/pallas_call | solution.py:501
  4.7 42.0 %scan.1.in_ref.inz_ref = f32[1088,128]{1,0:T(8,128)} custom-call(f32[1088,128]{1,0:T(8,128)} %get-tuple-element.15.own_ref, f32[16,128]{1,0:T(8,128)} %get-tuple-element.16.co_ref), custom_call_target="tpu_custom_call" | custom-call | tf_op jit(solution)/shard_map/scan/pallas_call | solution.py:513
  46.7 73.4 %middle.1 = (f32[32,128,128]{2,1,0:T(8,128)}, f32[1088,128]{1,0:T(8,128)}, f32[1088,128]{1,0:T(8,128)}, f32[256,1024]{1,0:T(8,128)}) custom-call(s32[1,8]{1,0:T(1,128)} %spans_ref.5, bf16[256,4096]{1,0:T(8,128)(2,1)} %bitcast.12, bf16[256,4096]{1,0:T(8,128)(2,1)} %bitcast.13, bf16[256,512]{1,0:T(8,128)(2,1)} %bitcast.8, ...), custom_call_target="tpu_custom_call" | custom-call | tf_op jit(solution)/shard_map/middle/pallas_call | solution.py:528
  120.1 73.8 %last.1 = (f32[4096,128]{1,0:T(8,128)}, f32[512,128]{1,0:T(8,128)}) custom-call(s32[1,8]{1,0:T(1,128)} %spans_ref.5, f32[1088,128]{1,0:T(8,128)} %get-tuple-element.17.own_ref, f32[16,128]{1,0:T(8,128)} %get-tuple-element.16.co_ref, f32[1088,128]{1,0:T(8,128)} %get-tuple-element.18.back1_ref, f32[256,1024]{1,0:T(8,128)} %get-tuple-element.19.dfk_ref, ...), custom_call_target="tpu_custom_call" | custom-call | tf_op jit(solution)/shard_map/last/pallas_call | solution.py:561
  193.8 0.0 copy-start
  193.9 3.2 %copy.11 = f32[32,128,128]{2,1,0:T(8,128)} copy(f32[32,128,128]{2,1,0:T(8,128)} %bitcast.11) | data formatting | bytes 4194304
  197.0 0.0 copy-done
  197.0 0.7 copy.12
Async XLA Ops:
  193.8 3.2 %copy-start = (f32[512,128]{1,0:T(8,128)S(1)}, f32[512,128]{1,0:T(8,128)}, u32[]{:S(2)}) copy-start(f32[512,128]{1,0:T(8,128)} %get-tuple-element.23) | copy-start | bytes 786436

commit v2 on v1

--- a/solution.py
+++ b/solution.py
@@ -234,9 +234,17 @@
     scan.finish()
 
 
+def softmax_pair_t(u):
+    e1 = jnp.exp(u - jnp.max(u, 0, keepdims=True))
+    e2 = jnp.exp(jnp.min(u, 0, keepdims=True) - u)
+    p1 = e1 * (1.0 / jnp.sum(e1, 0, keepdims=True))
+    p2 = e2 * (1.0 / jnp.sum(e2, 0, keepdims=True))
+    return p1, p2
+
+
 def middle_kernel(
     coef, spans_ref, q_ref, t_ref, v_ref, fk_ref, w_ref, st0_ref, st0z_ref, in_ref, inz_ref,
-    gq_ref, back_ref, back1_ref, dfk_ref, fq_s, x_s, p_s, m_s,
+    gq_ref, back_ref, back1_ref, dfk_ref, f_s, x_s, p_s, m_s, both_s,
 ):
     head = pl.program_id(0)
     block = pl.program_id(1)
@@ -248,61 +256,69 @@
     in1 = no_start(starts, b0, b0 + 1)
     w_in = jnp.where(block == 0, in0, in1)
     w_st = jnp.where(block == 0, 0.0, same)
+    top = lax.broadcasted_iota(jnp.int32, (16, 128), 0)
     m_s[0:128, :] = fk_ref[...]
-    zb = []
     for half in (0, 1):
         rows = slice(half * 128, (half + 1) * 128)
         m_s[128:256, rows] = (w_in * in_ref[rows, :] + w_st * st0_ref[rows, :]).astype(BF16)
         zr = pl.ds(2 * head + half, 1)
-        zb.append((w_in * inz_ref[zr, :] + w_st * st0z_ref[zr, :]).astype(BF16).astype(F32))
-    m = m_s[...]
+        zb = w_in * inz_ref[zr, :] + w_st * st0z_ref[zr, :]
+        m_s[256:272, rows] = jnp.where(top == 0, zb, 0.0).astype(BF16)
     v = v_ref[...]
-    causal = lax.broadcasted_iota(jnp.int32, (SPAN, SPAN), 0) >= lax.broadcasted_iota(
+    causal = lax.broadcasted_iota(jnp.int32, (SPAN, SPAN), 0) <= lax.broadcasted_iota(
         jnp.int32, (SPAN, SPAN), 1
     )
-    gz = [jnp.zeros((8, 128), F32), jnp.zeros((8, 128), F32)]
     for g in range(GROUP):
         cols = slice(g * HD, (g + 1) * HD)
-        rows = slice(g * SPAN, (g + 1) * SPAN)
-        q = q_ref[:, cols]
-        p1, p2 = softmax_pair(dot(q, w_ref[g], 1, 0))
-        f1 = p1.astype(BF16)
-        f2 = p2.astype(BF16)
-        fq_s[rows, 0:128] = f1
-        fq_s[rows, 128:256] = f2
-        p_s[g % 2, 0] = p1
-        p_s[g % 2, 1] = p2
-        both = dot(fq_s[rows, :], m, 1, 1)
-        scores = jnp.where(causal, both[:, 0:128], 0.0)
-        f1 = f1.astype(F32)
-        f2 = f2.astype(F32)
-        den = jnp.sum(scores + f1 * zb[0] + f2 * zb[1], -1, keepdims=True)
-        inv = 1.0 / den
-        num = dot(scores.astype(BF16), v, 1, 0) + both[:, 128:256]
-        out = num * inv
-        dy = coef * (out - t_ref[:, cols].astype(F32))
-        dnum = (dy * inv).astype(BF16)
-        dden = -jnp.sum(dy * out, -1, keepdims=True) * inv
-        pairs = jnp.where(causal, dot(dnum, v, 1, 1) + dden, 0.0).astype(BF16)
-        x_s[rows, 0:128] = pairs
-        x_s[rows, 128:256] = dnum
-        for half, f in ((0, f1), (1, f2)):
-            gz[half] = gz[half] + jnp.sum((f * dden).reshape(SPAN // 8, 8, 128), 0)
-        dfq = dot(x_s[rows, :], m, 1, 0)
-        duq = map_grad(
-            p_s[g % 2, 0], p_s[g % 2, 1], dfq[:, 0:128] + dden * zb[0], dfq[:, 128:256] + dden * zb[1]
-        )
-        grad = dot(q, duq, 0, 0)
-
-        @pl.when(block == 0)
-        def _():
-            gq_ref[g] = grad
-
-        @pl.when(block == 1)
-        def _():
-            gq_ref[g] = gq_ref[g] + grad
-
-    acc = dot(x_s[...], fq_s[...], 0, 0)
+        p1, p2 = softmax_pair_t(dot(w_ref[g], q_ref[:, cols], 0, 1))
+        f_s[0:128, cols] = p1.astype(BF16)
+        f_s[128:256, cols] = p2.astype(BF16)
+        p_s[0, :, cols] = p1
+        p_s[1, :, cols] = p2
+    both_s[...] = dot(m_s[...], f_s[...], 1, 0)
+    zcol = dot(m_s[256:272, :], jnp.ones((16, 128), BF16), 0, 0)
+    invs = []
+    for g in range(GROUP):
+        cols = slice(g * HD, (g + 1) * HD)
+        scores = jnp.where(causal, both_s[0:128, cols], 0.0)
+        x_s[0:128, cols] = scores.astype(BF16)
+        invs.append(1.0 / (jnp.sum(scores, 0, keepdims=True) + both_s[256:257, cols]))
+    both_s[128:256, :] = both_s[128:256, :] + dot(v, x_s[0:128, :], 0, 0)
+    eye = (
+        lax.broadcasted_iota(jnp.int32, (HD, HD), 0) == lax.broadcasted_iota(jnp.int32, (HD, HD), 1)
+    ).astype(F32).astype(BF16)
+    ddens = []
+    for g in range(GROUP):
+        cols = slice(g * HD, (g + 1) * HD)
+        inv = invs[g]
+        out = both_s[128:256, cols] * inv
+        dy = coef * (out - dot(eye, t_ref[:, cols], 1, 1))
+        x_s[128:256, cols] = (dy * inv).astype(BF16)
+        dden = -jnp.sum(dy * out, 0, keepdims=True) * inv
+        ddens.append(dden)
+        hi = dden.astype(BF16).astype(F32)
+        mid = (dden - hi).astype(BF16).astype(F32)
+        low = dden - hi - mid
+        x_s[256:272, cols] = jnp.where(
+            top == 0, hi, jnp.where(top == 1, mid, jnp.where(top == 2, low, 0.0))
+        ).astype(BF16)
+    both_s[0:128, :] = dot(v, x_s[128:256, :], 1, 0)
+    for g in range(GROUP):
+        cols = slice(g * HD, (g + 1) * HD)
+        x_s[0:128, cols] = jnp.where(causal, both_s[0:128, cols] + ddens[g], 0.0).astype(BF16)
+    both_s[0:256, :] = dot(m_s[0:256, :], x_s[0:256, :], 0, 0)
+    for g in range(GROUP):
+        cols = slice(g * HD, (g + 1) * HD)
+        p1, p2 = p_s[0, :, cols], p_s[1, :, cols]
+        d1 = both_s[0:128, cols] + zcol[0:128] * ddens[g]
+        d2 = both_s[128:256, cols] + zcol[128:256] * ddens[g]
+        s1 = jnp.sum(p1 * d1, 0, keepdims=True)
+        s2 = jnp.sum(p2 * d2, 0, keepdims=True)
+        duq = (p1 * (d1 - s1) - p2 * (d2 - s2)).astype(BF16)
+        grad = dot(q_ref[:, cols], duq, 0, 1)
+        gq_ref[g] = jnp.where(block == 0, 0.0, gq_ref[g]) + grad
+
+    acc = dot(x_s[...], f_s[...], 1, 1)
     dfk_ref[...] = acc[0:128, :]
 
     @pl.when(jnp.logical_and(head == 0, block == 0))
@@ -311,8 +327,9 @@
         back1_ref[pl.ds(ZROW, ROWS - ZROW), :] = jnp.zeros((ROWS - ZROW, 128), F32)
 
     for half in (0, 1):
-        part = acc[128:256, half * 128 : (half + 1) * 128]
-        zpart = jnp.sum(gz[half], 0, keepdims=True)
+        lanes = slice(half * 128, (half + 1) * 128)
+        part = acc[128:256, lanes]
+        zpart = acc[256:257, lanes] + acc[257:258, lanes] + acc[258:259, lanes]
         rows = pl.ds(pl.multiple_of(head * 256 + half * 128, 128), 128)
         zr = pl.ds(ZROW + 2 * head + half, 1)
 
@@ -546,10 +563,11 @@
             pl.BlockSpec((SPAN, 256), lambda i, c: (c, i)),
         ),
         scratch_shapes=[
-            pltpu.VMEM((GROUP * SPAN, 256), BF16),
-            pltpu.VMEM((GROUP * SPAN, 256), BF16),
-            pltpu.VMEM((2, 2, SPAN, 128), F32),
-            pltpu.VMEM((256, 256), BF16),
+            pltpu.VMEM((256, GROUP * SPAN), BF16),
+            pltpu.VMEM((272, GROUP * SPAN), BF16),
+            pltpu.VMEM((2, 128, GROUP * SPAN), F32),
+            pltpu.VMEM((272, 256), BF16),
+            pltpu.VMEM((272, GROUP * SPAN), F32),
         ],
         compiler_params=pltpu.CompilerParams(
             dimension_semantics=("arbitrary", "arbitrary"), vmem_limit_bytes=LIMIT

time: 199 us -> 148 us (0.74)
  Pallas kernels: 193 us -> 142 us
    pallas_call x1, Pallas kernels: 73.4 us -> 22.3 us  [shards(): pl.pallas_call(functools.partial(middle_kernel, coef), grid=(HK, 2), out_...]
where the time goes in v2:
time: 148 us; the launch traced here: 147 us
  Pallas kernels  142 us (96%)
  local copies, waits for them, and re-layouts  3.88 us (3%)
    pallas_call x1, Pallas kernels, shards(): pl.pallas_call(last_kernel, out_shape=(shape((HK * GROUP * HD, HD)), shap...  73.8 us
    pallas_call x1, Pallas kernels, shards(): pl.pallas_call(state_kernel, out_shape=shape((ROWS, 128)), in_specs=[VM,...  42 us
    pallas_call x1, Pallas kernels, shards(): pl.pallas_call(functools.partial(middle_kernel, coef), grid=(HK, 2), out_...  22.3 us
    pallas_call x1, Pallas kernels, shards(): pl.pallas_call(key_kernel, out_shape=(shape((toks, HK * 256), BF16), shap...  4.07 us
    unnamed x4, local copies, waits for them, and re-layouts  3.88 us

profile of v2, /device:TPU:1, one launch (start us, length us, event | category | flops | bytes accessed | tf_op | source)
XLA Modules:
  0.0 146.7 jit_solution(9034524675026878418)
XLA Ops:
  0.6 4.1 %keys.1 = (bf16[256,1024]{1,0:T(8,128)(2,1)}, f32[2,256,512]{2,1,0:T(8,128)}, f32[1088,128]{1,0:T(8,128)}, f32[1088,128]{1,0:T(8,128)}, f32[16,128]{1,0:T(8,128)}) custom-call(s32[1,8]{1,0:T(1,128)} %spans_ref.5, bf16[256,512]{1,0:T(8,128)(2,1)} %bitcast.14, bf16[256,512]{1,0:T(8,128)(2,1)} %bitcast.7, bf16[4,128,128]{2,1,0:T(8,128)(2,1)} %w_ref.2), custom_call_target="tpu_custom_call" | custom-call | tf_op jit(solution)/shard_map/keys/pallas_call | solution.py:518
  4.7 42.0 %scan.1.in_ref.inz_ref = f32[1088,128]{1,0:T(8,128)} custom-call(f32[1088,128]{1,0:T(8,128)} %get-tuple-element.15.own_ref, f32[16,128]{1,0:T(8,128)} %get-tuple-element.16.co_ref), custom_call_target="tpu_custom_call" | custom-call | tf_op jit(solution)/shard_map/scan/pallas_call | solution.py:530
  46.7 22.3 %middle.1 = (f32[32,128,128]{2,1,0:T(8,128)}, f32[1088,128]{1,0:T(8,128)}, f32[1088,128]{1,0:T(8,128)}, f32[256,1024]{1,0:T(8,128)}) custom-call(s32[1,8]{1,0:T(1,128)} %spans_ref.5, bf16[256,4096]{1,0:T(8,128)(2,1)} %bitcast.12, bf16[256,4096]{1,0:T(8,128)(2,1)} %bitcast.13, bf16[256,512]{1,0:T(8,128)(2,1)} %bitcast.8, ...), custom_call_target="tpu_custom_call" | custom-call | tf_op jit(solution)/shard_map/middle/pallas_call | solution.py:545
  69.0 73.8 %last.1 = (f32[4096,128]{1,0:T(8,128)}, f32[512,128]{1,0:T(8,128)}) custom-call(s32[1,8]{1,0:T(1,128)} %spans_ref.5, f32[1088,128]{1,0:T(8,128)} %get-tuple-element.17.own_ref, f32[16,128]{1,0:T(8,128)} %get-tuple-element.16.co_ref, f32[1088,128]{1,0:T(8,128)} %get-tuple-element.18.back1_ref, f32[256,1024]{1,0:T(8,128)} %get-tuple-element.19.dfk_ref, ...), custom_call_target="tpu_custom_call" | custom-call | tf_op jit(solution)/shard_map/last/pallas_call | solution.py:579
  142.8 0.0 copy-start
  142.8 3.2 %copy.11 = f32[32,128,128]{2,1,0:T(8,128)} copy(f32[32,128,128]{2,1,0:T(8,128)} %bitcast.11) | data formatting | bytes 4194304
  146.0 0.0 copy-done
  146.0 0.7 copy.12
Async XLA Ops:
  142.8 3.2 %copy-start = (f32[512,128]{1,0:T(8,128)S(1)}, f32[512,128]{1,0:T(8,128)}, u32[]{:S(2)}) copy-start(f32[512,128]{1,0:T(8,128)} %get-tuple-element.23) | copy-start | bytes 786436

commit v3 on v0

v3 whole, which is shorter than its diff:
```python
import functools
import math

import jax
import jax.numpy as jnp
from jax import lax
from jax.experimental import pallas as pl
from jax.experimental.pallas import tpu as pltpu
from jax.sharding import PartitionSpec as P

MESH = pl.DeviceIdType.MESH
F32 = jnp.float32
BF16 = jnp.bfloat16
SPAN = 128
HD = 128
HK = 4
GROUP = 8
NDOC = 8
NZ = 8
NY = 4
NDP = 8
ZROW = 256
FIRST, LAST = 0, HK - 1


def dot(a, b, ca, cb):
    return lax.dot_general(a, b, (((ca,), (cb,)), ((), ())), preferred_element_type=F32)


def starts_of(spans_ref):
    starts, total = [], jnp.int32(0)
    for n in range(NDOC):
        starts.append(total)
        total = total + spans_ref[0, n]
    return starts


def no_start(starts, *blocks):
    hit = jnp.bool_(False)
    for s in starts:
        for b in blocks:
            hit = jnp.logical_or(hit, s == b)
    return jnp.where(hit, 0.0, 1.0).astype(F32)


def softmax_pair(u):
    e1 = jnp.exp(u - jnp.max(u, -1, keepdims=True))
    e2 = jnp.exp(jnp.min(u, -1, keepdims=True) - u)
    p1 = e1 * (1.0 / jnp.sum(e1, -1, keepdims=True))
    p2 = e2 * (1.0 / jnp.sum(e2, -1, keepdims=True))
    return p1, p2


def map_grad(p1, p2, d1, d2):
    s1 = jnp.sum(p1 * d1, -1, keepdims=True)
    s2 = jnp.sum(p2 * d2, -1, keepdims=True)
    return (p1 * (d1 - s1) - p2 * (d2 - s2)).astype(BF16)


def softmax_pair_t(u):
    e1 = jnp.exp(u - jnp.max(u, 0, keepdims=True))
    e2 = jnp.exp(jnp.min(u, 0, keepdims=True) - u)
    p1 = e1 * (1.0 / jnp.sum(e1, 0, keepdims=True))
    p2 = e2 * (1.0 / jnp.sum(e2, 0, keepdims=True))
    return p1, p2


def remote(src, dst, send, recv, dev):
    return pltpu.make_async_remote_copy(
        src_ref=src, dst_ref=dst, send_sem=send, recv_sem=recv, device_id=dev, device_id_type=MESH
    )


def send_all(items):
    copies = [remote(*item) for item in items]
    for copy in copies:
        copy.start()
    return copies


def rows_of(index, size):
    return pl.ds(pl.multiple_of(index * size, 8), size)


def slice_rows(head, holder):
    return 40 if head == holder else 32


def scan_scratch(holder):
    shapes = []
    for head in range(HK):
        size = slice_rows(head, holder)
        shapes += [
            pltpu.VMEM((NZ * size, 128), F32),
            pltpu.VMEM((NZ * size, 128), F32),
            pltpu.VMEM((NZ, size, 128), F32),
            pltpu.VMEM((size, 128), F32),
            pltpu.VMEM((2, size, 128), F32),
            pltpu.VMEM((NZ, size, 128), F32),
            pltpu.SemaphoreType.DMA((2, NZ)),
            pltpu.SemaphoreType.DMA((2, 2)),
            pltpu.SemaphoreType.DMA((2, NZ)),
        ]
    return shapes


class Scan:
    def __init__(self, at, co, scratch, size, reverse):
        self.co, self.size, self.reverse = co, size, reverse
        self.own, self.out, self.seen, self.total, self.rows_in, self.back = scratch[:6]
        self.s1, self.s2, self.s3 = scratch[6:]
        self.dp, self.seq, self.y, self.z = at
        self.order = list(range(NZ))[::-1] if reverse else list(range(NZ))

    def start(self):
        self.copies = send_all([
            (
                self.own.at[rows_of(lax.rem(self.z + d, NZ), self.size)], self.seen.at[self.z],
                self.s1.at[0, d], self.s1.at[1, d], (self.dp, self.y * NZ + lax.rem(self.z + d, NZ)),
            )
            for d in range(1, NZ)
        ])

    def totals(self):
        self.seen[self.z] = self.own[rows_of(self.z, self.size), :]
        for copy in self.copies:
            copy.wait_recv()
        acc = jnp.zeros((self.size, 128), F32)
        for k in self.order:
            self.back[k] = acc
            acc = self.seen[k] + self.co[k : k + 1, :] * acc
        self.total[...] = acc
        self.row_copies = send_all([
            (
                self.total, self.rows_in.at[d - 1], self.s2.at[0, d - 1], self.s2.at[1, d - 1],
                (self.dp, lax.rem(self.y + (NY - d if self.reverse else d), NY) * NZ + self.z),
            )
            for d in (1, 2)
        ])

    def give_back(self):
        for copy in self.row_copies:
            copy.wait_recv()
        first = 10 if self.reverse else 8
        carry = (
            self.co[first : first + 1, :] * self.rows_in[0]
            + self.co[first + 1 : first + 2, :] * self.rows_in[1]
        )
        keep = jnp.ones((1, 128), F32)
        for k in self.order:
            self.back[k] = self.back[k] + keep * carry
            keep = keep * self.co[k : k + 1, :]
        self.out[rows_of(self.z, self.size), :] = self.back[self.z]
        self.back_copies = send_all([
            (
                self.back.at[lax.rem(self.z + d, NZ)], self.out.at[rows_of(self.z, self.size)],
                self.s3.at[0, d], self.s3.at[1, d], (self.dp, self.y * NZ + lax.rem(self.z + d, NZ)),
            )
            for d in range(1, NZ)
        ])

    def arrived(self):
        for copy in self.back_copies:
            copy.wait_recv()

    def sent(self):
        return self.copies + self.row_copies + self.back_copies


def sum_scratch():
    dma = pltpu.SemaphoreType.DMA
    return [
        pltpu.VMEM((1024, 128), F32), pltpu.VMEM((1024, 128), F32), pltpu.VMEM((16, 64, 128), F32),
        pltpu.VMEM((64, 128), F32), pltpu.VMEM((NZ, 8, 128), F32),
        dma((2,)), dma((2, 16)), dma((2, NZ)), dma((2, NZ)), dma((2, 16)), dma((2,)),
    ]


class Total:
    def __init__(self, at, part, source, out, scratch, mate, planes, zs):
        self.source, self.out = source, out
        self.half_in, self.half, self.xy_in, self.quarter, self.z_in = scratch[:5]
        self.sc, self.sxy, self.sz, self.az, self.axy, self.ac = scratch[5:]
        self.mate, self.planes, self.zs = mate, planes, zs
        self.dp, self.seq, self.y, self.z = at
        self.x, self.core = lax.div(self.dp, 2), lax.rem(self.dp, 2)
        self.low = part * 2048
        self.base = self.low + self.core * 1024 + (self.x * 4 + self.y) * 64

    def core_rows(self, core):
        return pl.ds(pl.multiple_of(self.low + core * 1024, 8), 1024)

    def pair(self):
        self.c1 = send_all([
            (self.source.at[self.core_rows(1 - self.core)], self.half_in, self.sc.at[0], self.sc.at[1], self.mate)
        ])

    def plane(self):
        self.c1[0].wait_recv()
        self.half[...] = self.source[self.core_rows(self.core), :] + self.half_in[...]
        items = []
        for d in range(1, 16):
            spot = lax.rem(self.x + d // 4, 4) * 4 + lax.rem(self.y + d % 4, 4)
            items.append((
                self.half.at[rows_of(spot, 64)], self.xy_in.at[d], self.sxy.at[0, d], self.sxy.at[1, d],
                self.planes[d - 1],
            ))
        self.c2 = send_all(items)

    def along_z(self):
        for copy in self.c2:
            copy.wait_recv()
        acc = self.half[rows_of(self.x * 4 + self.y, 64), :]
        for d in range(1, 16):
            acc = acc + self.xy_in[d]
        self.quarter[...] = acc
        self.c3 = send_all([
            (
                self.quarter.at[rows_of(lax.rem(self.z + d, NZ), 8)], self.z_in.at[d],
                self.sz.at[0, d], self.sz.at[1, d], self.zs[d - 1],
            )
            for d in range(1, NZ)
        ])

    def back_z(self):
        for copy in self.c3:
            copy.wait_recv()
        acc = self.quarter[rows_of(self.z, 8), :]
        for d in range(1, NZ):
            acc = acc + self.z_in[d]
        mine = pl.ds(pl.multiple_of(self.base + self.z * 8, 8), 8)
        self.out[mine, :] = acc
        self.c4 = send_all([
            (self.out.at[mine], self.out.at[mine], self.az.at[0, d], self.az.at[1, d], self.zs[d - 1])
            for d in range(1, NZ)
        ])

    def back_plane(self):
        for copy in self.c4:
            copy.wait_recv()
        block = pl.ds(pl.multiple_of(self.base, 8), 64)
        self.c5 = send_all([
            (self.out.at[block], self.out.at[block], self.axy.at[0, d], self.axy.at[1, d], self.planes[d - 1])
            for d in range(1, 16)
        ])

    def back_pair(self):
        for copy in self.c5:
            copy.wait_recv()
        whole = self.core_rows(self.core)
        self.c6 = send_all([(self.out.at[whole], self.out.at[whole], self.ac.at[0], self.ac.at[1], self.mate)])

    def arrived(self):
        self.c6[0].wait_recv()

    def sent(self):
        return self.c1 + self.c2 + self.c3 + self.c4 + self.c5 + self.c6


N_SCAN = 9 * HK
N_SUM = 11


def whole_kernel(
    coef, spans_ref, q_hbm, k_ref, v_ref, t_hbm, w_hbm, wk_ref, oq_ref, ok_ref,
    q_s, t_s, w_s, fk_s, pk_s, st0_s, st0z_s, co_s, p_s, f_s, x_s, m_s, both_s, d_s, acc_s, gq_s,
    gk, kd_in, kd, ky_in, ky, kz_in, load, skd, sky, skz, aky, akd, *scratch,
):
    dp, seq = lax.axis_index("dp"), lax.axis_index("seq")
    y, z = lax.div(seq, NZ), lax.rem(seq, NZ)
    at = (dp, seq, y, z)
    x, core = lax.div(dp, 2), lax.rem(dp, 2)
    mate = (x * 2 + (1 - core), seq)
    zs = [(dp, y * NZ + lax.rem(z + d, NZ)) for d in range(1, NZ)]
    ys = [(dp, lax.rem(y + d, NY) * NZ + z) for d in range(1, NY)]
    dps = [(lax.rem(dp + d, NDP), seq) for d in range(1, NDP)]
    planes = [
        (lax.rem(x + d // 4, 4) * 2 + core, lax.rem(y + d % 4, 4) * NZ + z) for d in range(1, 16)
    ]
    other = [(lax.rem(x + d, 4) * 2 + (1 - core), seq) for d in range(4)]
    peers = zs + planes + other
    barrier = pltpu.get_barrier_semaphore()
    for dev in peers:
        pl.semaphore_signal(barrier, inc=1, device_id=dev, device_id_type=MESH)

    loads = []
    for h in range(HK):
        lanes = pl.ds(h * GROUP * HD, GROUP * HD)
        maps = pl.ds(h * GROUP, GROUP)
        loads.append([
            pltpu.make_async_copy(q_hbm.at[:, lanes], q_s.at[:, lanes], load.at[0, h]),
            pltpu.make_async_copy(w_hbm.at[maps], w_s.at[maps], load.at[1, h]),
            pltpu.make_async_copy(t_hbm.at[:, lanes], t_s.at[:, lanes], load.at[2, h]),
        ])
    for kind in range(3):
        for h in range(HK):
            loads[h][kind].start()

    starts = starts_of(spans_ref)
    b0 = 2 * seq
    in0 = no_start(starts, b0)
    same = no_start(starts, b0 + 1)
    in1 = no_start(starts, b0, b0 + 1)
    out0 = no_start(starts, b0 + 1, b0 + 2)
    out1 = no_start(starts, b0 + 2)
    halves = [(0, slice(0, 128)), (1, slice(128, 256))]

    fwd = [
        Scan(at, co_s, scratch[9 * h : 9 * h + 9], slice_rows(h, FIRST), False) for h in range(HK)
    ]
    rest = scratch[N_SCAN:]
    rev = [Scan(at, co_s, rest[9 * h : 9 * h + 9], slice_rows(h, LAST), True) for h in range(HK)]
    rest = rest[N_SCAN:]
    sums = [
        Total(at, p, gq_s, oq_ref, rest[N_SUM * p : N_SUM * p + N_SUM], mate, planes, zs) for p in (0, 1)
    ]

    fwd[FIRST].own[pl.ds(ZROW, 64), :] = jnp.zeros((64, 128), F32)
    rev[LAST].own[pl.ds(ZROW, 64), :] = jnp.zeros((64, 128), F32)
    for h in range(HK):
        cols = slice(h * HD, (h + 1) * HD)
        p1, p2 = softmax_pair(dot(k_ref[:, cols], wk_ref[h], 1, 0))
        pk_s[0, :, cols] = p1
        pk_s[1, :, cols] = p2
        fk = jnp.concatenate([p1, p2], -1).astype(BF16)
        fk_s[:, h * 256 : (h + 1) * 256] = fk
        v = v_ref[:, cols]
        toks = [slice(c * SPAN, (c + 1) * SPAN) for c in (0, 1)]
        st = [dot(v[r], fk[r], 0, 0) for r in toks]
        zsum = [jnp.sum(fk[r].astype(F32), 0, keepdims=True) for r in toks]
        for half, lanes in halves:
            rows = slice(half * 128, (half + 1) * 128)
            st0_s[h, rows, :] = st[0][:, lanes]
            fwd[h].own[rows, :] = same * st[0][:, lanes] + st[1][:, lanes]
            n = 2 * h + half
            st0z_s[n : n + 1, :] = zsum[0][:, lanes]
            fwd[FIRST].own[ZROW + n : ZROW + n + 1, :] = same * zsum[0][:, lanes] + zsum[1][:, lanes]
    pos = lax.broadcasted_iota(jnp.int32, (NZ, 128), 0) + y * NZ
    hit = jnp.zeros((NZ, 128), F32)
    before, after = jnp.float32(1.0), jnp.float32(1.0)
    for s in starts:
        hit = jnp.where(pos == s // 2, 1.0, hit)
        before = jnp.where(s // 16 == y - 1, 0.0, before)
        after = jnp.where(s // 16 == y + 1, 0.0, after)
    co_s[0:8, :] = 1.0 - hit
    co_s[8:9, :] = jnp.full((1, 128), jnp.where(y >= 1, 1.0, 0.0), F32)
    co_s[9:10, :] = jnp.full((1, 128), jnp.where(y >= 2, before, 0.0), F32)
    co_s[10:11, :] = jnp.full((1, 128), jnp.where(y <= 2, 1.0, 0.0), F32)
    co_s[11:12, :] = jnp.full((1, 128), jnp.where(y <= 1, after, 0.0), F32)

    pl.semaphore_wait(barrier, len(peers))
    for h in range(HK):
        fwd[h].start()

    def features(h):
        loads[h][0].wait()
        loads[h][1].wait()
        for g in range(GROUP):
            cols = slice((h * GROUP + g) * HD, (h * GROUP + g + 1) * HD)
            spot = slice(g * SPAN, (g + 1) * SPAN)
            p1, p2 = softmax_pair_t(dot(w_s[h * GROUP + g], q_s[:, cols], 0, 1))
            for c in (0, 1):
                toks = slice(c * SPAN, (c + 1) * SPAN)
                f_s[2 * h + c, 0:128, spot] = p1[:, toks].astype(BF16)
                f_s[2 * h + c, 128:256, spot] = p2[:, toks].astype(BF16)
                p_s[2 * h + c, 0, :, spot] = p1[:, toks]
                p_s[2 * h + c, 1, :, spot] = p2[:, toks]

    top = lax.broadcasted_iota(jnp.int32, (16, 128), 0)
    down = lax.broadcasted_iota(jnp.int32, (SPAN, SPAN), 0)
    across = lax.broadcasted_iota(jnp.int32, (SPAN, SPAN), 1)
    causal = down <= across
    eye = (down == across).astype(F32).astype(BF16)

    def middle(h):
        loads[h][2].wait()

        def one_block(c, carry):
            w_in = jnp.where(c == 0, in0, in1)
            w_st = jnp.where(c == 0, 0.0, same)
            toks = pl.ds(pl.multiple_of(c * SPAN, SPAN), SPAN)
            ic = 2 * h + c
            m_s[0:128, :] = fk_s[toks, h * 256 : (h + 1) * 256]
            for half, lanes in halves:
                rows = slice(half * 128, (half + 1) * 128)
                m_s[128:256, lanes] = (w_in * fwd[h].out[rows, :] + w_st * st0_s[h, rows, :]).astype(BF16)
                n = 2 * h + half
                zb = w_in * fwd[FIRST].out[ZROW + n : ZROW + n + 1, :] + w_st * st0z_s[n : n + 1, :]
                m_s[256:272, lanes] = jnp.where(top == 0, zb, 0.0).astype(BF16)
            v = v_ref[toks, h * HD : (h + 1) * HD]
            both_s[...] = dot(m_s[...], f_s[ic], 1, 0)
            zcol = dot(m_s[256:272, :], jnp.ones((16, 128), BF16), 0, 0)
            invs = []
            for g in range(GROUP):
                spot = slice(g * SPAN, (g + 1) * SPAN)
                scores = jnp.where(causal, both_s[0:128, spot], 0.0)
                x_s[0:128, spot] = scores.astype(BF16)
                invs.append(1.0 / (jnp.sum(scores, 0, keepdims=True) + both_s[256:257, spot]))
            both_s[128:256, :] = both_s[128:256, :] + dot(v, x_s[0:128, :], 0, 0)
            ddens = []
            for g in range(GROUP):
                cols = slice((h * GROUP + g) * HD, (h * GROUP + g + 1) * HD)
                spot = slice(g * SPAN, (g + 1) * SPAN)
                inv = invs[g]
                out = both_s[128:256, spot] * inv
                dy = coef * (out - dot(eye, t_s[toks, cols], 1, 1))
                x_s[128:256, spot] = (dy * inv).astype(BF16)
                dden = -jnp.sum(dy * out, 0, keepdims=True) * inv
                ddens.append(dden)
                hi = dden.astype(BF16).astype(F32)
                mid = (dden - hi).astype(BF16).astype(F32)
                low = dden - hi - mid
                x_s[256:272, spot] = jnp.where(
                    top == 0, hi, jnp.where(top == 1, mid, jnp.where(top == 2, low, 0.0))
                ).astype(BF16)
            both_s[0:128, :] = dot(v, x_s[128:256, :], 1, 0)
            for g in range(GROUP):
                spot = slice(g * SPAN, (g + 1) * SPAN)
                x_s[0:128, spot] = jnp.where(causal, both_s[0:128, spot] + ddens[g], 0.0).astype(BF16)
            both_s[0:256, :] = dot(m_s[0:256, :], x_s[0:256, :], 0, 0)
            for g in range(GROUP):
                spot = slice(g * SPAN, (g + 1) * SPAN)
                p1, p2 = p_s[ic, 0, :, spot], p_s[ic, 1, :, spot]
                d1 = both_s[0:128, spot] + zcol[0:128] * ddens[g]
                d2 = both_s[128:256, spot] + zcol[128:256] * ddens[g]
                s1 = jnp.sum(p1 * d1, 0, keepdims=True)
                s2 = jnp.sum(p2 * d2, 0, keepdims=True)
                d_s[c, :, spot] = (p1 * (d1 - s1) - p2 * (d2 - s2)).astype(BF16)
            acc_s[ic] = dot(x_s[...], f_s[ic], 1, 1)
            return carry

        lax.fori_loop(0, 2, one_block, 0)
        for g in range(GROUP):
            n = h * GROUP + g
            cols = slice(n * HD, (n + 1) * HD)
            spot = slice(g * SPAN, (g + 1) * SPAN)
            gq_s[n * HD : (n + 1) * HD, :] = dot(q_s[0:SPAN, cols], d_s[0, :, spot], 0, 1) + dot(
                q_s[SPAN : 2 * SPAN, cols], d_s[1, :, spot], 0, 1
            )
        for half, lanes in halves:
            rows = slice(half * 128, (half + 1) * 128)
            rev[h].own[rows, :] = in0 * acc_s[2 * h, 128:256, lanes] + in1 * acc_s[2 * h + 1, 128:256, lanes]
            gz = [sum_rows(acc_s, 2 * h + c, lanes) for c in (0, 1)]
            n = 2 * h + half
            rev[LAST].own[ZROW + n : ZROW + n + 1, :] = in0 * gz[0] + in1 * gz[1]

    a, b = sums
    features(0)
    features(1)
    fwd[0].totals()
    features(2)
    fwd[0].give_back()
    fwd[1].totals()
    features(3)
    fwd[1].give_back()
    fwd[2].totals()
    fwd[2].give_back()
    fwd[3].totals()
    fwd[3].give_back()

    fwd[0].arrived()
    middle(0)
    rev[0].start()
    fwd[1].arrived()
    middle(1)
    rev[1].start()
    a.pair()
    rev[0].totals()
    fwd[2].arrived()
    middle(2)
    rev[2].start()
    rev[0].give_back()
    rev[1].totals()
    a.plane()
    fwd[3].arrived()
    middle(3)
    rev[3].start()
    b.pair()
    rev[1].give_back()
    rev[2].totals()
    b.plane()
    a.along_z()
    rev[2].give_back()
    a.back_z()
    rev[3].totals()
    a.back_plane()
    b.along_z()
    rev[3].give_back()
    b.back_z()
    a.back_pair()
    for h in range(HK):
        rev[h].arrived()

    for h in range(HK):
        cols = slice(h * HD, (h + 1) * HD)
        total = jnp.zeros((HD, HD), F32)
        for c in (0, 1):
            toks = slice(c * SPAN, (c + 1) * SPAN)
            grads = []
            for half, lanes in halves:
                rows = slice(half * 128, (half + 1) * 128)
                zr = slice(ZROW + 2 * h + half, ZROW + 2 * h + half + 1)
                r, rz = rev[h].out[rows, :], rev[LAST].out[zr, :]
                if c == 0:
                    r = same * acc_s[2 * h + 1, 128:256, lanes] + out0 * r
                    rz = same * sum_rows(acc_s, 2 * h + 1, lanes) + out0 * rz
                else:
                    r, rz = out1 * r, out1 * rz
                grads.append(
                    acc_s[2 * h + c, 0:128, lanes] + dot(v_ref[toks, cols], r.astype(BF16), 1, 0)
                    + rz.astype(BF16).astype(F32)
                )
            duk = map_grad(pk_s[0, toks, cols], pk_s[1, toks, cols], grads[0], grads[1])
            total = total + dot(k_ref[toks, cols], duk, 0, 0)
        gk[cols, :] = total
    kdsend = send_all([
        (gk.at[rows_of(lax.rem(dp + d, NDP), 64)], kd_in.at[d], skd.at[0, d], skd.at[1, d], dps[d - 1])
        for d in range(1, NDP)
    ])
    b.back_plane()
    for copy in kdsend:
        copy.wait_recv()
    acc = gk[rows_of(dp, 64), :]
    for d in range(1, NDP):
        acc = acc + kd_in[d]
    kd[...] = acc
    kysend = send_all([
        (kd.at[rows_of(lax.rem(y + d, NY), 16)], ky_in.at[d], sky.at[0, d], sky.at[1, d], ys[d - 1])
        for d in range(1, NY)
    ])
    for copy in kysend:
        copy.wait_recv()
    acc = kd[rows_of(y, 16), :]
    for d in range(1, NY):
        acc = acc + ky_in[d]
    ky[...] = acc
    kz_in[z] = acc
    kzsend = send_all([
        (ky, kz_in.at[z], skz.at[0, d], skz.at[1, d], zs[d - 1]) for d in range(1, NZ)
    ])
    b.back_pair()
    for copy in kzsend:
        copy.wait_recv()
    acc = kz_in[0]
    for n in range(1, NZ):
        acc = acc + kz_in[n]
    kmine = pl.ds(pl.multiple_of(dp * 64 + y * 16, 8), 16)
    ok_ref[kmine, :] = acc
    kyback = send_all([
        (ok_ref.at[kmine], ok_ref.at[kmine], aky.at[0, d], aky.at[1, d], ys[d - 1]) for d in range(1, NY)
    ])
    for copy in kyback:
        copy.wait_recv()
    kblock = rows_of(dp, 64)
    kdback = send_all([
        (ok_ref.at[kblock], ok_ref.at[kblock], akd.at[0, d], akd.at[1, d], dps[d - 1])
        for d in range(1, NDP)
    ])
    a.arrived()
    b.arrived()
    for copy in kdback:
        copy.wait_recv()
    for part in fwd + rev + sums:
        for copy in part.sent():
            copy.wait_send()
    for copy in kdsend + kysend + kzsend + kyback + kdback:
        copy.wait_send()


def sum_rows(acc_s, index, lanes):
    return acc_s[index, 256:257, lanes] + acc_s[index, 257:258, lanes] + acc_s[index, 258:259, lanes]


VM = pl.BlockSpec(memory_space=pltpu.VMEM)
SM = pl.BlockSpec(memory_space=pltpu.SMEM)
ANY = pl.BlockSpec(memory_space=pl.ANY)
LIMIT = 60 * 1024 * 1024


def shards(queries, keys, values, targets, q_map, k_map, doc_spans):
    toks = queries.shape[1]
    heads = HK * GROUP
    coef = 2.0 / math.sqrt(lax.axis_size("dp") * lax.axis_size("seq") * toks * HD)
    dma = pltpu.SemaphoreType.DMA
    vmem = pltpu.VMEM
    gq, gk = pl.pallas_call(
        functools.partial(whole_kernel, coef),
        out_shape=(
            jax.ShapeDtypeStruct((heads * HD, HD), F32), jax.ShapeDtypeStruct((HK * HD, HD), F32),
        ),
        in_specs=[SM, ANY, VM, VM, ANY, ANY, VM],
        out_specs=(VM, VM),
        scratch_shapes=[
            vmem((toks, heads * HD), BF16),
            vmem((toks, heads * HD), BF16),
            vmem((heads, HD, HD), BF16),
            vmem((toks, HK * 256), BF16),
            vmem((2, toks, HK * HD), F32),
            vmem((HK, 256, 128), F32),
            vmem((8, 128), F32),
            vmem((16, 128), F32),
            vmem((2 * HK, 2, 128, GROUP * SPAN), F32),
            vmem((2 * HK, 256, GROUP * SPAN), BF16),
            vmem((272, GROUP * SPAN), BF16),
            vmem((272, 256), BF16),
            vmem((272, GROUP * SPAN), F32),
            vmem((2, HD, GROUP * SPAN), BF16),
            vmem((2 * HK, 272, 256), F32),
            vmem((heads * HD, HD), F32),
            vmem((HK * HD, HD), F32),
            vmem((NDP, 64, 128), F32),
            vmem((64, 128), F32),
            vmem((NY, 16, 128), F32),
            vmem((16, 128), F32),
            vmem((NZ, 16, 128), F32),
            dma((3, HK)),
            dma((2, NDP)), dma((2, NY)), dma((2, NZ)), dma((2, NY)), dma((2, NDP)),
        ] + scan_scratch(FIRST) + scan_scratch(LAST) + sum_scratch() + sum_scratch(),
        compiler_params=pltpu.CompilerParams(
            collective_id=0, has_side_effects=True, vmem_limit_bytes=LIMIT
        ),
        name="whole",
    )(doc_spans, queries[0], keys[0], values[0], targets[0], q_map, k_map)
    return gq.reshape(heads, HD, HD), gk.reshape(HK, HD, HD)


def solution(mesh):
    placed = (
        P("dp", "seq", None), P("dp", "seq", None), P("dp", "seq", None), P("dp", "seq", None),
        P(), P(), P("dp", None),
    )
    return jax.shard_map(shards, mesh=mesh, in_specs=placed, out_specs=(P(), P()), check_vma=False)
```

time: 461 us -> 112 us (0.24); the launches traced: 452 us -> 111 us
  blocking collectives: 222 us -> 0 us
  Pallas kernels: 0 us -> 107 us
  matrix products: 56.9 us -> 0 us
  other arithmetic: 51.4 us -> 0 us
  local copies, waits for them, and re-layouts: 47.9 us -> 3.88 us
  waiting for transfers between devices: 39.9 us -> 0 us
  between operations: 33.9 us -> 0.65 us
    all_to_all x2 -> x0, blocking collectives: 112 us -> none  [the longest x1 59.3 us: sent_to_all(): return lax.all_to_all(copies, axis, split_axis=0, concat_axis=0, tiled=True)]
    pallas_call x0 -> x1, Pallas kernels: none -> 107 us  [shards(): pl.pallas_call(functools.partial(whole_kernel, coef), out_shape=(jax.Shap...]
    all_gather x5 -> x0, blocking collectives: 82.8 us -> none  [the longest x4 57.2 us: carried_in_2(): pieces = jax.tree.map(lambda part: lax.all_gather(part, axis), total)]
    dot_general x22 -> x0, matrix products: 54.1 us -> none  [the longest x8 14.9 us: spread_blocks(): jnp.einsum('cy,y...->c...', weights, blocks, precision=lax.Precision.HIGH...]
    all_gather x4 -> x0, waiting for transfers between devices: 39.8 us -> none  [carried_in_2(): pieces = jax.tree.map(lambda part: lax.all_gather(part, axis), total)]
    unnamed x2 -> x0, blocking collectives: 27 us -> none
    div x4 -> x0, other arithmetic: 15.6 us -> none  [the longest x1 7.88 us: hedgehog(): upper = jax.nn.softmax(mapped, axis=-1)]
    unnamed x92 -> x4, local copies, waits for them, and re-layouts: 15.2 us -> 3.88 us
  transfers between devices with their start and end apart: 4 -> 0, of which waited for: 1 -> 0; matrix products, arithmetic and copies ran while one was open for 22% -> 0% of each run, Pallas kernels for 0% -> 0%
where the time goes in v3:
time: 112 us; the launch traced here: 111 us
  Pallas kernels  107 us (96%)
  local copies, waits for them, and re-layouts  3.88 us (3%)
    pallas_call x1, Pallas kernels, shards(): pl.pallas_call(functools.partial(whole_kernel, coef), out_shape=(jax.Shap...  107 us
    unnamed x4, local copies, waits for them, and re-layouts  3.88 us

profile of v3, /device:TPU:1, one launch (start us, length us, event | category | flops | bytes accessed | tf_op | source)
XLA Modules:
  0.0 111.5 jit_solution(13677258379147723659)
XLA Ops:
  0.6 106.9 %whole.1 = (f32[4096,128]{1,0:T(8,128)}, f32[512,128]{1,0:T(8,128)}) custom-call(s32[1,8]{1,0:T(1,128)} %spans_ref.1, bf16[256,4096]{1,0:T(8,128)(2,1)} %bitcast.6, bf16[256,512]{1,0:T(8,128)(2,1)} %bitcast.9, bf16[256,512]{1,0:T(8,128)(2,1)} %bitcast.10, bf16[256,4096]{1,0:T(8,128)(2,1)} %bitcast.7, bf16[32,128,128]{2,1,0:T(8,128)(2,1)} %w_hbm.1, ...), custom_call_target="tpu_custom_call" | custom-call | tf_op jit(solution)/shard_map/whole/pallas_call | solution.py:586
  107.6 0.0 copy-start
  107.6 3.2 %copy.11 = f32[32,128,128]{2,1,0:T(8,128)} copy(f32[32,128,128]{2,1,0:T(8,128)} %bitcast.8) | data formatting | bytes 4194304
  110.8 0.0 copy-done
  110.8 0.7 copy.12
Async XLA Ops:
  107.6 3.2 %copy-start = (f32[512,128]{1,0:T(8,128)S(1)}, f32[512,128]{1,0:T(8,128)}, u32[]{:S(2)}) copy-start(f32[512,128]{1,0:T(8,128)} %get-tuple-element.5) | copy-start | bytes 786436

commit v4 on v3

--- a/solution.py
+++ b/solution.py
@@ -263,8 +263,8 @@
 
 def whole_kernel(
     coef, spans_ref, q_hbm, k_ref, v_ref, t_hbm, w_hbm, wk_ref, oq_ref, ok_ref,
-    q_s, t_s, w_s, fk_s, pk_s, st0_s, st0z_s, co_s, p_s, f_s, x_s, m_s, both_s, d_s, acc_s, gq_s,
-    gk, kd_in, kd, ky_in, ky, kz_in, load, skd, sky, skz, aky, akd, *scratch,
+    q_s, t_s, w_s, fk_s, pk_s, st0_s, st0z_s, co_s, p_s, f_s, x_s, m_s, both_s, d_s, acc_s, gq_s, den_s, num_s,
+    gk, kd_in, ky, kz_in, load, skd, skz, akd, *scratch,
 ):
     dp, seq = lax.axis_index("dp"), lax.axis_index("seq")
     y, z = lax.div(seq, NZ), lax.rem(seq, NZ)
@@ -272,13 +272,13 @@
     x, core = lax.div(dp, 2), lax.rem(dp, 2)
     mate = (x * 2 + (1 - core), seq)
     zs = [(dp, y * NZ + lax.rem(z + d, NZ)) for d in range(1, NZ)]
-    ys = [(dp, lax.rem(y + d, NY) * NZ + z) for d in range(1, NY)]
-    dps = [(lax.rem(dp + d, NDP), seq) for d in range(1, NDP)]
     planes = [
         (lax.rem(x + d // 4, 4) * 2 + core, lax.rem(y + d % 4, 4) * NZ + z) for d in range(1, 16)
     ]
-    other = [(lax.rem(x + d, 4) * 2 + (1 - core), seq) for d in range(4)]
-    peers = zs + planes + other
+    layer = [
+        (lax.rem(dp + d // NY, NDP), lax.rem(y + d % NY, NY) * NZ + z) for d in range(1, NDP * NY)
+    ]
+    peers = zs + layer
     barrier = pltpu.get_barrier_semaphore()
     for dev in peers:
         pl.semaphore_signal(barrier, inc=1, device_id=dev, device_id_type=MESH)
@@ -372,6 +372,21 @@
     causal = down <= across
     eye = (down == across).astype(F32).astype(BF16)
 
+    def local(h):
+        def one_block(c, carry):
+            toks = pl.ds(pl.multiple_of(c * SPAN, SPAN), SPAN)
+            ic = 2 * h + c
+            both_s[0:128, :] = dot(fk_s[toks, h * 256 : (h + 1) * 256], f_s[ic], 1, 0)
+            for g in range(GROUP):
+                spot = slice(g * SPAN, (g + 1) * SPAN)
+                scores = jnp.where(causal, both_s[0:128, spot], 0.0)
+                x_s[0:128, spot] = scores.astype(BF16)
+                den_s[ic, 0:1, spot] = jnp.sum(scores, 0, keepdims=True)
+            num_s[ic] = dot(v_ref[toks, h * HD : (h + 1) * HD], x_s[0:128, :], 0, 0)
+            return carry
+
+        lax.fori_loop(0, 2, one_block, 0)
+
     def middle(h):
         loads[h][2].wait()
 
@@ -388,21 +403,14 @@
                 zb = w_in * fwd[FIRST].out[ZROW + n : ZROW + n + 1, :] + w_st * st0z_s[n : n + 1, :]
                 m_s[256:272, lanes] = jnp.where(top == 0, zb, 0.0).astype(BF16)
             v = v_ref[toks, h * HD : (h + 1) * HD]
-            both_s[...] = dot(m_s[...], f_s[ic], 1, 0)
+            both_s[128:272, :] = dot(m_s[128:272, :], f_s[ic], 1, 0)
             zcol = dot(m_s[256:272, :], jnp.ones((16, 128), BF16), 0, 0)
-            invs = []
-            for g in range(GROUP):
-                spot = slice(g * SPAN, (g + 1) * SPAN)
-                scores = jnp.where(causal, both_s[0:128, spot], 0.0)
-                x_s[0:128, spot] = scores.astype(BF16)
-                invs.append(1.0 / (jnp.sum(scores, 0, keepdims=True) + both_s[256:257, spot]))
-            both_s[128:256, :] = both_s[128:256, :] + dot(v, x_s[0:128, :], 0, 0)
             ddens = []
             for g in range(GROUP):
                 cols = slice((h * GROUP + g) * HD, (h * GROUP + g + 1) * HD)
                 spot = slice(g * SPAN, (g + 1) * SPAN)
-                inv = invs[g]
-                out = both_s[128:256, spot] * inv
+                inv = 1.0 / (den_s[ic, 0:1, spot] + both_s[256:257, spot])
+                out = (num_s[ic, :, spot] + both_s[128:256, spot]) * inv
                 dy = coef * (out - dot(eye, t_s[toks, cols], 1, 1))
                 x_s[128:256, spot] = (dy * inv).astype(BF16)
                 dden = -jnp.sum(dy * out, 0, keepdims=True) * inv
@@ -449,15 +457,18 @@
     features(1)
     fwd[0].totals()
     features(2)
+    local(0)
     fwd[0].give_back()
     fwd[1].totals()
     features(3)
     fwd[1].give_back()
     fwd[2].totals()
+    local(1)
+    fwd[3].totals()
     fwd[2].give_back()
-    fwd[3].totals()
+    local(2)
     fwd[3].give_back()
-
+    local(3)
     fwd[0].arrived()
     middle(0)
     rev[0].start()
@@ -465,20 +476,20 @@
     middle(1)
     rev[1].start()
     a.pair()
-    rev[0].totals()
     fwd[2].arrived()
+    a.plane()
     middle(2)
     rev[2].start()
-    rev[0].give_back()
-    rev[1].totals()
-    a.plane()
+    rev[0].totals()
     fwd[3].arrived()
     middle(3)
     rev[3].start()
     b.pair()
+    rev[1].totals()
+    rev[0].give_back()
+    b.plane()
+    rev[2].totals()
     rev[1].give_back()
-    rev[2].totals()
-    b.plane()
     a.along_z()
     rev[2].give_back()
     a.back_z()
@@ -487,7 +498,6 @@
     b.along_z()
     rev[3].give_back()
     b.back_z()
-    a.back_pair()
     for h in range(HK):
         rev[h].arrived()
 
@@ -514,48 +524,36 @@
             total = total + dot(k_ref[toks, cols], duk, 0, 0)
         gk[cols, :] = total
     kdsend = send_all([
-        (gk.at[rows_of(lax.rem(dp + d, NDP), 64)], kd_in.at[d], skd.at[0, d], skd.at[1, d], dps[d - 1])
-        for d in range(1, NDP)
+        (
+            gk.at[rows_of(lax.rem(dp + d // NY, NDP) * NY + lax.rem(y + d % NY, NY), 16)], kd_in.at[d],
+            skd.at[0, d], skd.at[1, d], layer[d - 1],
+        )
+        for d in range(1, NDP * NY)
     ])
-    b.back_plane()
+    a.back_pair()
     for copy in kdsend:
         copy.wait_recv()
-    acc = gk[rows_of(dp, 64), :]
-    for d in range(1, NDP):
+    acc = gk[rows_of(dp * NY + y, 16), :]
+    for d in range(1, NDP * NY):
         acc = acc + kd_in[d]
-    kd[...] = acc
-    kysend = send_all([
-        (kd.at[rows_of(lax.rem(y + d, NY), 16)], ky_in.at[d], sky.at[0, d], sky.at[1, d], ys[d - 1])
-        for d in range(1, NY)
-    ])
-    for copy in kysend:
-        copy.wait_recv()
-    acc = kd[rows_of(y, 16), :]
-    for d in range(1, NY):
-        acc = acc + ky_in[d]
     ky[...] = acc
     kz_in[z] = acc
     kzsend = send_all([
         (ky, kz_in.at[z], skz.at[0, d], skz.at[1, d], zs[d - 1]) for d in range(1, NZ)
     ])
-    b.back_pair()
+    b.back_plane()
     for copy in kzsend:
         copy.wait_recv()
     acc = kz_in[0]
     for n in range(1, NZ):
         acc = acc + kz_in[n]
-    kmine = pl.ds(pl.multiple_of(dp * 64 + y * 16, 8), 16)
+    kmine = rows_of(dp * NY + y, 16)
     ok_ref[kmine, :] = acc
-    kyback = send_all([
-        (ok_ref.at[kmine], ok_ref.at[kmine], aky.at[0, d], aky.at[1, d], ys[d - 1]) for d in range(1, NY)
+    kdback = send_all([
+        (ok_ref.at[kmine], ok_ref.at[kmine], akd.at[0, d], akd.at[1, d], layer[d - 1])
+        for d in range(1, NDP * NY)
     ])
-    for copy in kyback:
-        copy.wait_recv()
-    kblock = rows_of(dp, 64)
-    kdback = send_all([
-        (ok_ref.at[kblock], ok_ref.at[kblock], akd.at[0, d], akd.at[1, d], dps[d - 1])
-        for d in range(1, NDP)
-    ])
+    b.back_pair()
     a.arrived()
     b.arrived()
     for copy in kdback:
@@ -563,7 +561,7 @@
     for part in fwd + rev + sums:
         for copy in part.sent():
             copy.wait_send()
-    for copy in kdsend + kysend + kzsend + kyback + kdback:
+    for copy in kdsend + kzsend + kdback:
         copy.wait_send()
 
 
@@ -574,7 +572,7 @@
 VM = pl.BlockSpec(memory_space=pltpu.VMEM)
 SM = pl.BlockSpec(memory_space=pltpu.SMEM)
 ANY = pl.BlockSpec(memory_space=pl.ANY)
-LIMIT = 60 * 1024 * 1024
+LIMIT = 51200 * 1024
 
 
 def shards(queries, keys, values, targets, q_map, k_map, doc_spans):
@@ -607,14 +605,14 @@
             vmem((2, HD, GROUP * SPAN), BF16),
             vmem((2 * HK, 272, 256), F32),
             vmem((heads * HD, HD), F32),
+            vmem((2 * HK, 8, GROUP * SPAN), F32),
+            vmem((2 * HK, HD, GROUP * SPAN), F32),
             vmem((HK * HD, HD), F32),
-            vmem((NDP, 64, 128), F32),
-            vmem((64, 128), F32),
-            vmem((NY, 16, 128), F32),
+            vmem((NDP * NY, 16, 128), F32),
             vmem((16, 128), F32),
             vmem((NZ, 16, 128), F32),
             dma((3, HK)),
-            dma((2, NDP)), dma((2, NY)), dma((2, NZ)), dma((2, NY)), dma((2, NDP)),
+            dma((2, NDP * NY)), dma((2, NZ)), dma((2, NDP * NY)),
         ] + scan_scratch(FIRST) + scan_scratch(LAST) + sum_scratch() + sum_scratch(),
         compiler_params=pltpu.CompilerParams(
             collective_id=0, has_side_effects=True, vmem_limit_bytes=LIMIT

time: 112 us -> 105 us (0.938)
  Pallas kernels: 107 us -> 97 us
  local copies, waits for them, and re-layouts: 3.88 us -> 6.7 us
    pallas_call x1, Pallas kernels: 107 us -> 97 us  [shards(): pl.pallas_call(functools.partial(whole_kernel, coef), out_shape=(jax.Shap...]
    unnamed x4 -> x12, local copies, waits for them, and re-layouts: 3.88 us -> 6.7 us
where the time goes in v4:
time: 105 us; the launch traced here: 104 us
  Pallas kernels  97 us (92%)
  local copies, waits for them, and re-layouts  6.7 us (6%)
    pallas_call x1, Pallas kernels, shards(): pl.pallas_call(functools.partial(whole_kernel, coef), out_shape=(jax.Shap...  97 us
    unnamed x12, local copies, waits for them, and re-layouts  6.7 us

profile of v4, /device:TPU:1, one launch (start us, length us, event | category | flops | bytes accessed | tf_op | source)
XLA Modules:
  0.0 104.4 jit_solution(17931024802632275208)
XLA Ops:
  0.6 0.0 copy-start
  0.6 1.2 %copy-done = bf16[32,128,128]{2,1,0:T(8,128)(2,1)S(1)} copy-done((bf16[32,128,128]{2,1,0:T(8,128)(2,1)S(1)}, bf16[32,128,128]{2,1,0:T(8,128)(2,1)}, u32[]{:S(2)}) %copy-start) | copy-done | bytes 1048600
  1.9 0.0 copy-start.1
  1.9 0.9 copy-done.1
  2.8 0.0 copy-start.2
  2.8 0.9 copy-done.2
  3.8 0.0 copy-start.3
  3.8 0.9 copy-done.3
  4.7 0.0 copy-start.4
  4.7 0.7 copy-done.4
  5.3 97.0 %whole.1 = (f32[4096,128]{1,0:T(8,128)S(1)}, f32[512,128]{1,0:T(8,128)S(1)}) custom-call(s32[1,8]{1,0:T(1,128)S(1)} %copy-done.4, bf16[256,4096]{1,0:T(8,128)(2,1)} %bitcast.10, bf16[256,512]{1,0:T(8,128)(2,1)S(1)} %bitcast.7, bf16[256,512]{1,0:T(8,128)(2,1)S(1)} %bitcast.8, bf16[256,4096]{1,0:T(8,128)(2,1)} %bitcast.11, bf16[32,128,128]{2,1,0:T(8,128)(2,1)S(1)} %copy-done, ...), custom_call_target="tpu_custom_call" | custom-call | tf_op jit(solution)/shard_map/whole/pallas_call | solution.py:584
  102.3 1.3 %copy.11 = f32[32,128,128]{2,1,0:T(8,128)} copy(f32[32,128,128]{2,1,0:T(8,128)S(1)} %bitcast.6) | data formatting | bytes 4194304
  103.7 0.7 copy.12
Async XLA Ops:
  0.6 1.2 %copy-start = (bf16[32,128,128]{2,1,0:T(8,128)(2,1)S(1)}, bf16[32,128,128]{2,1,0:T(8,128)(2,1)}, u32[]{:S(2)}) copy-start(bf16[32,128,128]{2,1,0:T(8,128)(2,1)} %w_hbm.1) | copy-start | bytes 3145732
  1.9 0.9 copy-start.1
  2.8 0.9 copy-start.2
  3.8 0.9 copy-start.3
  4.7 0.7 copy-start.4

commit v5 on v4

--- a/solution.py
+++ b/solution.py
@@ -455,20 +455,20 @@
     a, b = sums
     features(0)
     features(1)
-    fwd[0].totals()
     features(2)
     local(0)
+    fwd[0].totals()
+    features(3)
+    fwd[1].totals()
     fwd[0].give_back()
-    fwd[1].totals()
-    features(3)
+    local(1)
+    fwd[2].totals()
     fwd[1].give_back()
-    fwd[2].totals()
-    local(1)
+    local(2)
     fwd[3].totals()
     fwd[2].give_back()
-    local(2)
+    local(3)
     fwd[3].give_back()
-    local(3)
     fwd[0].arrived()
     middle(0)
     rev[0].start()
@@ -485,18 +485,18 @@
     middle(3)
     rev[3].start()
     b.pair()
+    a.along_z()
     rev[1].totals()
     rev[0].give_back()
     b.plane()
     rev[2].totals()
     rev[1].give_back()
-    a.along_z()
     rev[2].give_back()
+    rev[3].totals()
     a.back_z()
-    rev[3].totals()
-    a.back_plane()
     b.along_z()
     rev[3].give_back()
+    a.back_plane()
     b.back_z()
     for h in range(HK):
         rev[h].arrived()
@@ -569,10 +569,34 @@
     return acc_s[index, 256:257, lanes] + acc_s[index, 257:258, lanes] + acc_s[index, 258:259, lanes]
 
 
+OUT_PARTS = 8
+
+
+def store_kernel(a_ref, b_ref, oa_ref, ob_ref, a_s, b_s, sems):
+    part = a_s.shape[0] // OUT_PARTS
+    pieces = [(a_ref, a_s, oa_ref, pl.ds(n * part, part)) for n in range(OUT_PARTS)]
+    pieces.append((b_ref, b_s, ob_ref, pl.ds(0, b_s.shape[0])))
+    into = [
+        pltpu.make_async_copy(src.at[r], held.at[r], sems.at[0, n])
+        for n, (src, held, _, r) in enumerate(pieces)
+    ]
+    out = [
+        pltpu.make_async_copy(held.at[r], dst.at[r], sems.at[1, n])
+        for n, (_, held, dst, r) in enumerate(pieces)
+    ]
+    for copy in into:
+        copy.start()
+    for n in range(len(pieces)):
+        into[n].wait()
+        out[n].start()
+    for copy in out:
+        copy.wait()
+
+
 VM = pl.BlockSpec(memory_space=pltpu.VMEM)
 SM = pl.BlockSpec(memory_space=pltpu.SMEM)
 ANY = pl.BlockSpec(memory_space=pl.ANY)
-LIMIT = 51200 * 1024
+LIMIT = 60 * 1024 * 1024
 
 
 def shards(queries, keys, values, targets, q_map, k_map, doc_spans):
@@ -619,7 +643,18 @@
         ),
         name="whole",
     )(doc_spans, queries[0], keys[0], values[0], targets[0], q_map, k_map)
-    return gq.reshape(heads, HD, HD), gk.reshape(HK, HD, HD)
+    gq, gk = pl.pallas_call(
+        store_kernel,
+        out_shape=(
+            jax.ShapeDtypeStruct((heads, HD, HD), F32), jax.ShapeDtypeStruct((HK, HD, HD), F32),
+        ),
+        in_specs=[ANY, ANY],
+        out_specs=(ANY, ANY),
+        scratch_shapes=[vmem((heads, HD, HD), F32), vmem((HK, HD, HD), F32), dma((2, OUT_PARTS + 1))],
+        compiler_params=pltpu.CompilerParams(vmem_limit_bytes=LIMIT),
+        name="store",
+    )(gq.reshape(heads, HD, HD), gk.reshape(HK, HD, HD))
+    return gq, gk
 
 
 def solution(mesh):

time: 105 us -> 99.1 us (0.944)
  local copies, waits for them, and re-layouts: 6.7 us -> 0 us
  Pallas kernels: 97 us -> 98.1 us
    unnamed x12 -> x0, local copies, waits for them, and re-layouts: 6.7 us -> none
    pallas_call x0 -> x1, Pallas kernels: none -> 2.5 us  [shards(): pl.pallas_call(store_kernel, out_shape=(jax.ShapeDtypeStruct((heads, HD,...]
    pallas_call x1, Pallas kernels: 97 us -> 95.6 us  [shards(): pl.pallas_call(functools.partial(whole_kernel, coef), out_shape=(jax.Shap...]
where the time goes in v5:
time: 99.1 us; the launch traced here: 98.9 us
  Pallas kernels  98.1 us (99%)
    pallas_call x1, Pallas kernels, shards(): pl.pallas_call(functools.partial(whole_kernel, coef), out_shape=(jax.Shap...  95.6 us
    pallas_call x1, Pallas kernels, shards(): pl.pallas_call(store_kernel, out_shape=(jax.ShapeDtypeStruct((heads, HD,...  2.5 us

profile of v5, /device:TPU:1, one launch (start us, length us, event | category | flops | bytes accessed | tf_op | source)
XLA Modules:
  0.0 98.9 jit_solution(16757996538670962064)
XLA Ops:
  0.6 95.6 %whole.1 = (f32[4096,128]{1,0:T(8,128)}, f32[512,128]{1,0:T(8,128)}) custom-call(s32[1,8]{1,0:T(1,128)} %spans_ref.1, bf16[256,4096]{1,0:T(8,128)(2,1)} %bitcast.6, bf16[256,512]{1,0:T(8,128)(2,1)} %bitcast.9, bf16[256,512]{1,0:T(8,128)(2,1)} %bitcast.10, bf16[256,4096]{1,0:T(8,128)(2,1)} %bitcast.7, bf16[32,128,128]{2,1,0:T(8,128)(2,1)} %w_hbm.1, ...), custom_call_target="tpu_custom_call" | custom-call | tf_op jit(solution)/shard_map/whole/pallas_call | solution.py:608
  96.3 2.5 %store.1 = (f32[32,128,128]{2,1,0:T(8,128)}, f32[4,128,128]{2,1,0:T(8,128)}) custom-call(f32[32,128,128]{2,1,0:T(8,128)} %bitcast.8, f32[4,128,128]{2,1,0:T(8,128)} %bitcast.11), custom_call_target="tpu_custom_call" | custom-call | tf_op jit(solution)/shard_map/store/pallas_call | solution.py:646

commit v6 on v5

--- a/solution.py
+++ b/solution.py
@@ -380,14 +380,14 @@
             for g in range(GROUP):
                 spot = slice(g * SPAN, (g + 1) * SPAN)
                 scores = jnp.where(causal, both_s[0:128, spot], 0.0)
-                x_s[0:128, spot] = scores.astype(BF16)
+                x_s[ic, 0:128, spot] = scores.astype(BF16)
                 den_s[ic, 0:1, spot] = jnp.sum(scores, 0, keepdims=True)
-            num_s[ic] = dot(v_ref[toks, h * HD : (h + 1) * HD], x_s[0:128, :], 0, 0)
+            num_s[ic] = dot(v_ref[toks, h * HD : (h + 1) * HD], x_s[ic, 0:128, :], 0, 0)
             return carry
 
         lax.fori_loop(0, 2, one_block, 0)
 
-    def middle(h):
+    def front(h):
         loads[h][2].wait()
 
         def one_block(c, carry):
@@ -395,46 +395,59 @@
             w_st = jnp.where(c == 0, 0.0, same)
             toks = pl.ds(pl.multiple_of(c * SPAN, SPAN), SPAN)
             ic = 2 * h + c
-            m_s[0:128, :] = fk_s[toks, h * 256 : (h + 1) * 256]
+            m_s[ic, 0:128, :] = fk_s[toks, h * 256 : (h + 1) * 256]
             for half, lanes in halves:
                 rows = slice(half * 128, (half + 1) * 128)
-                m_s[128:256, lanes] = (w_in * fwd[h].out[rows, :] + w_st * st0_s[h, rows, :]).astype(BF16)
+                m_s[ic, 128:256, lanes] = (w_in * fwd[h].out[rows, :] + w_st * st0_s[h, rows, :]).astype(BF16)
                 n = 2 * h + half
                 zb = w_in * fwd[FIRST].out[ZROW + n : ZROW + n + 1, :] + w_st * st0z_s[n : n + 1, :]
-                m_s[256:272, lanes] = jnp.where(top == 0, zb, 0.0).astype(BF16)
+                m_s[ic, 256:272, lanes] = jnp.where(top == 0, zb, 0.0).astype(BF16)
             v = v_ref[toks, h * HD : (h + 1) * HD]
-            both_s[128:272, :] = dot(m_s[128:272, :], f_s[ic], 1, 0)
-            zcol = dot(m_s[256:272, :], jnp.ones((16, 128), BF16), 0, 0)
-            ddens = []
+            both_s[128:272, :] = dot(m_s[ic, 128:272, :], f_s[ic], 1, 0)
             for g in range(GROUP):
                 cols = slice((h * GROUP + g) * HD, (h * GROUP + g + 1) * HD)
                 spot = slice(g * SPAN, (g + 1) * SPAN)
                 inv = 1.0 / (den_s[ic, 0:1, spot] + both_s[256:257, spot])
                 out = (num_s[ic, :, spot] + both_s[128:256, spot]) * inv
                 dy = coef * (out - dot(eye, t_s[toks, cols], 1, 1))
-                x_s[128:256, spot] = (dy * inv).astype(BF16)
+                x_s[ic, 128:256, spot] = (dy * inv).astype(BF16)
                 dden = -jnp.sum(dy * out, 0, keepdims=True) * inv
-                ddens.append(dden)
+                den_s[ic, 1:2, spot] = dden
                 hi = dden.astype(BF16).astype(F32)
                 mid = (dden - hi).astype(BF16).astype(F32)
                 low = dden - hi - mid
-                x_s[256:272, spot] = jnp.where(
+                x_s[ic, 256:272, spot] = jnp.where(
                     top == 0, hi, jnp.where(top == 1, mid, jnp.where(top == 2, low, 0.0))
                 ).astype(BF16)
-            both_s[0:128, :] = dot(v, x_s[128:256, :], 1, 0)
+            both_s[0:128, :] = dot(v, x_s[ic, 128:256, :], 1, 0)
             for g in range(GROUP):
                 spot = slice(g * SPAN, (g + 1) * SPAN)
-                x_s[0:128, spot] = jnp.where(causal, both_s[0:128, spot] + ddens[g], 0.0).astype(BF16)
-            both_s[0:256, :] = dot(m_s[0:256, :], x_s[0:256, :], 0, 0)
+                x_s[ic, 0:128, spot] = jnp.where(causal, both_s[0:128, spot] + den_s[ic, 1:2, spot], 0.0).astype(BF16)
+            acc_s[ic] = dot(x_s[ic], f_s[ic], 1, 1)
+            return carry
+
+        lax.fori_loop(0, 2, one_block, 0)
+        for half, lanes in halves:
+            rows = slice(half * 128, (half + 1) * 128)
+            rev[h].own[rows, :] = in0 * acc_s[2 * h, 128:256, lanes] + in1 * acc_s[2 * h + 1, 128:256, lanes]
+            gz = [sum_rows(acc_s, 2 * h + c, lanes) for c in (0, 1)]
+            n = 2 * h + half
+            rev[LAST].own[ZROW + n : ZROW + n + 1, :] = in0 * gz[0] + in1 * gz[1]
+
+    def rear(h):
+        def one_block(c, carry):
+            ic = 2 * h + c
+            zcol = dot(m_s[ic, 256:272, :], jnp.ones((16, 128), BF16), 0, 0)
+            both_s[0:256, :] = dot(m_s[ic, 0:256, :], x_s[ic, 0:256, :], 0, 0)
             for g in range(GROUP):
                 spot = slice(g * SPAN, (g + 1) * SPAN)
+                dden = den_s[ic, 1:2, spot]
                 p1, p2 = p_s[ic, 0, :, spot], p_s[ic, 1, :, spot]
-                d1 = both_s[0:128, spot] + zcol[0:128] * ddens[g]
-                d2 = both_s[128:256, spot] + zcol[128:256] * ddens[g]
+                d1 = both_s[0:128, spot] + zcol[0:128] * dden
+                d2 = both_s[128:256, spot] + zcol[128:256] * dden
                 s1 = jnp.sum(p1 * d1, 0, keepdims=True)
                 s2 = jnp.sum(p2 * d2, 0, keepdims=True)
                 d_s[c, :, spot] = (p1 * (d1 - s1) - p2 * (d2 - s2)).astype(BF16)
-            acc_s[ic] = dot(x_s[...], f_s[ic], 1, 1)
             return carry
 
         lax.fori_loop(0, 2, one_block, 0)
@@ -445,12 +458,6 @@
             gq_s[n * HD : (n + 1) * HD, :] = dot(q_s[0:SPAN, cols], d_s[0, :, spot], 0, 1) + dot(
                 q_s[SPAN : 2 * SPAN, cols], d_s[1, :, spot], 0, 1
             )
-        for half, lanes in halves:
-            rows = slice(half * 128, (half + 1) * 128)
-            rev[h].own[rows, :] = in0 * acc_s[2 * h, 128:256, lanes] + in1 * acc_s[2 * h + 1, 128:256, lanes]
-            gz = [sum_rows(acc_s, 2 * h + c, lanes) for c in (0, 1)]
-            n = 2 * h + half
-            rev[LAST].own[ZROW + n : ZROW + n + 1, :] = in0 * gz[0] + in1 * gz[1]
 
     a, b = sums
     features(0)
@@ -470,32 +477,36 @@
     local(3)
     fwd[3].give_back()
     fwd[0].arrived()
-    middle(0)
+    front(0)
     rev[0].start()
+    rear(0)
     fwd[1].arrived()
-    middle(1)
+    front(1)
     rev[1].start()
+    rear(1)
     a.pair()
     fwd[2].arrived()
+    front(2)
+    rev[2].start()
     a.plane()
-    middle(2)
-    rev[2].start()
     rev[0].totals()
     fwd[3].arrived()
-    middle(3)
+    front(3)
     rev[3].start()
-    b.pair()
-    a.along_z()
+    rear(2)
     rev[1].totals()
     rev[0].give_back()
-    b.plane()
+    rear(3)
+    b.pair()
     rev[2].totals()
     rev[1].give_back()
+    b.plane()
+    a.along_z()
     rev[2].give_back()
     rev[3].totals()
     a.back_z()
+    rev[3].give_back()
     b.along_z()
-    rev[3].give_back()
     a.back_plane()
     b.back_z()
     for h in range(HK):
@@ -623,8 +634,8 @@
             vmem((16, 128), F32),
             vmem((2 * HK, 2, 128, GROUP * SPAN), F32),
             vmem((2 * HK, 256, GROUP * SPAN), BF16),
-            vmem((272, GROUP * SPAN), BF16),
-            vmem((272, 256), BF16),
+            vmem((2 * HK, 272, GROUP * SPAN), BF16),
+            vmem((2 * HK, 272, 256), BF16),
             vmem((272, GROUP * SPAN), F32),
             vmem((2, HD, GROUP * SPAN), BF16),
             vmem((2 * HK, 272, 256), F32),

time: 99.1 us -> 99.3 us (level)
  no operation moved by 1% of the time
where the time goes in v6:
time: 99.3 us; the launch traced here: 99.2 us
  Pallas kernels  98.4 us (99%)
    pallas_call x1, Pallas kernels, shards(): pl.pallas_call(functools.partial(whole_kernel, coef), out_shape=(jax.Shap...  95.9 us
    pallas_call x1, Pallas kernels, shards(): pl.pallas_call(store_kernel, out_shape=(jax.ShapeDtypeStruct((heads, HD,...  2.5 us

profile of v6, /device:TPU:1, one launch (start us, length us, event | category | flops | bytes accessed | tf_op | source)
XLA Modules:
  0.0 99.2 jit_solution(5834219579507376559)
XLA Ops:
  0.6 95.9 %whole.1 = (f32[4096,128]{1,0:T(8,128)}, f32[512,128]{1,0:T(8,128)}) custom-call(s32[1,8]{1,0:T(1,128)} %spans_ref.1, bf16[256,4096]{1,0:T(8,128)(2,1)} %bitcast.6, bf16[256,512]{1,0:T(8,128)(2,1)} %bitcast.9, bf16[256,512]{1,0:T(8,128)(2,1)} %bitcast.10, bf16[256,4096]{1,0:T(8,128)(2,1)} %bitcast.7, bf16[32,128,128]{2,1,0:T(8,128)(2,1)} %w_hbm.1, ...), custom_call_target="tpu_custom_call" | custom-call | tf_op jit(solution)/shard_map/whole/pallas_call | solution.py:619
  96.5 2.5 %store.1 = (f32[32,128,128]{2,1,0:T(8,128)}, f32[4,128,128]{2,1,0:T(8,128)}) custom-call(f32[32,128,128]{2,1,0:T(8,128)} %bitcast.8, f32[4,128,128]{2,1,0:T(8,128)} %bitcast.11), custom_call_target="tpu_custom_call" | custom-call | tf_op jit(solution)/shard_map/store/pallas_call | solution.py:657
